TPU v7x, 32 devices: a whole 2x2x4 slice. The times are simulated.
32 devices in a mesh: dp: 8 (over z, x), tensor: 4 (over y, core).
Axes of the slice: x: 2, y: 2, z: 4, core: 2. Of those that a mesh axis runs over, the one named last changes fastest.
Arguments:
- tokens: bfloat16 [4096, 1024], P(('dp', 'tensor')), may hold values from -6 to 6
- seg_starts: int32 [8, 6], P('dp'), may hold values from 1 to 511, as said below
- norm1_gain: float32 [1024], replicated, may hold values from 0.5 to 1.5
- w_mix: bfloat16 [1024, 8, 768], P(None, 'tensor'), may hold values from -0.1875 to 0.1875
- w_gates: bfloat16 [1024, 8, 2], P(None, 'tensor'), may hold values from -0.1875 to 0.1875
- conv_w: float32 [4, 8, 512], P(None, 'tensor'), may hold values from -3 to 3
- decay_rate: float32 [8], P('tensor'), may hold values from 0.001 to 0.1
- onorm_gain: float32 [8, 256], P('tensor'), may hold values from 0.5 to 1.5
- w_out: bfloat16 [8, 256, 1024], P('tensor'), may hold values from -0.25 to 0.25
- norm2_gain: float32 [1024], replicated, may hold values from 0.5 to 1.5
- w_gu: bfloat16 [1024, 2, 2816], P(None, None, 'tensor'), may hold values from -0.1875 to 0.1875
- w_down: bfloat16 [2816, 1024], P('tensor'), may hold values from -0.21875 to 0.21875
- cotangent: bfloat16 [4096, 1024], P(('dp', 'tensor')), may hold values from -6 to 6
Outputs:
- output: bfloat16 [4096, 1024], P(('dp', 'tensor'))
- grad_tokens: bfloat16 [4096, 1024], P(('dp', 'tensor'))
- grad_norm1_gain: float32 [1024], P('dp')
- grad_w_mix: float32 [1024, 8, 768], P('dp', 'tensor')
- grad_w_gates: float32 [1024, 8, 2], P('dp', 'tensor')
- grad_conv_w: float32 [4, 8, 512], P(None, 'tensor')
- grad_decay_rate: float32 [8], P('tensor')
- grad_onorm_gain: float32 [8, 256], P('tensor')
- grad_w_out: float32 [8, 256, 1024], P('tensor', None, 'dp')
- grad_norm2_gain: float32 [1024], P('dp')
- grad_w_gu: float32 [1024, 2, 2816], P('dp', None, 'tensor')
- grad_w_down: float32 [2816, 1024], P('tensor', 'dp')
Inputs may be any that keep to these rules, and one draw needn't show every extreme that they name: `seg_starts`: each entry is a position where a document begins in that sequence; every row names one position twice.
All inputs are finite; a program needn't handle non-finite values.
Results may differ from a plain program's by a relative error of at most 0.024.
Values may be sent and summed in bfloat16 or wider, within the bound.
A program may use at most 128 MiB of HBM per device.

v0:
```python
import functools

import jax
import jax.numpy as jnp
from jax import lax
from jax.experimental import pallas as pl
from jax.experimental.pallas import tpu as pltpu
from jax.sharding import PartitionSpec as P

BLOCK = 64
HALO = 8
HI = lax.Precision.HIGHEST


def contract(a, b, dims, exact=False):
    if exact:
        return lax.dot_general(a, b, (dims, ((), ())), precision=HI, preferred_element_type=jnp.float32)
    a, b = a.astype(jnp.bfloat16), b.astype(jnp.bfloat16)
    return lax.dot_general(a, b, (dims, ((), ())), preferred_element_type=jnp.float32)


NN, NT, TN = ((1,), (0,)), ((1,), (1,)), ((0,), (0,))


@functools.partial(jax.custom_vjp, nondiff_argnums=(2,))
def mm_nn(a, b, exact=False):
    return contract(a, b, NN, exact)


mm_nn.defvjp(
    lambda a, b, exact: (contract(a, b, NN, exact), (a, b)),
    lambda exact, res, g: (contract(g, res[1], NT, exact), contract(res[0], g, TN, exact)),
)


@functools.partial(jax.custom_vjp, nondiff_argnums=(2,))
def mm_nt(a, b, exact=False):
    return contract(a, b, NT, exact)


mm_nt.defvjp(
    lambda a, b, exact: (contract(a, b, NT, exact), (a, b)),
    lambda exact, res, g: (contract(g, res[1], NN, exact), contract(g, res[0], TN, exact)),
)


@functools.partial(jax.custom_vjp, nondiff_argnums=(2,))
def mm_tn(a, b, exact=False):
    return contract(a, b, TN, exact)


mm_tn.defvjp(
    lambda a, b, exact: (contract(a, b, TN, exact), (a, b)),
    lambda exact, res, g: (contract(res[1], g, NT, exact), contract(res[0], g, NN, exact)),
)


@jax.custom_vjp
def solve(lower, rhs, inverse):
    return contract(inverse, rhs, NN)


def solve_fwd(lower, rhs, inverse):
    errs = contract(inverse, rhs, NN)
    return errs, (inverse, errs)


def solve_bwd(res, g):
    inverse, errs = res
    d_rhs = contract(inverse, g, TN)
    return -contract(d_rhs, errs, NT), d_rhs, jnp.zeros_like(inverse)


solve.defvjp(solve_fwd, solve_bwd)


@functools.partial(jax.custom_vjp, nondiff_argnums=(1,))
def keepsum(x, axis):
    return jnp.sum(x, axis=axis, keepdims=True)


keepsum.defvjp(
    lambda x, axis: (jnp.sum(x, axis=axis, keepdims=True), x),
    lambda axis, x, g: (jnp.broadcast_to(g, x.shape),),
)


@functools.partial(jax.custom_vjp, nondiff_argnums=(1,))
def spread(x, shape):
    return jnp.broadcast_to(x, shape)


def spread_bwd(shape, x, g):
    for axis in range(2):
        if x.shape[axis] == 1 and shape[axis] != 1:
            g = jnp.sum(g, axis=axis, keepdims=True)
    return (g,)


spread.defvjp(lambda x, shape: (jnp.broadcast_to(x, shape), x), spread_bwd)


@functools.partial(jax.custom_vjp, nondiff_argnums=(1,))
def lagged(ext, lag):
    return pltpu.roll(ext, lag, 0)[HALO:] if lag else ext[HALO:]


def lagged_bwd(lag, ext, g):
    full = jnp.concatenate([jnp.zeros((HALO, g.shape[1]), g.dtype), g], axis=0)
    return (pltpu.roll(full, full.shape[0] - lag, 0) if lag else full,)


lagged.defvjp(lambda ext, lag: (lagged(ext, lag), ext), lagged_bwd)


@jax.custom_vjp
def softplus(x):
    return jnp.maximum(x, 0.0) + jnp.log1p(jnp.exp(-jnp.abs(x)))


softplus.defvjp(lambda x: (softplus(x), x), lambda x, g: (g * jax.nn.sigmoid(x),))


def silu(x):
    return x * jax.nn.sigmoid(x)


def rms_norm(rows, gain):
    return rows * lax.rsqrt(jnp.mean(rows * rows, axis=-1, keepdims=True) + 1e-06) * gain


def segment_ids(starts_row, length):
    places = jnp.arange(length, dtype=jnp.int32)
    flags = jnp.any(starts_row[:, None] == places[None, :], axis=0).astype(jnp.int32)
    seg = jnp.cumsum(flags)
    before = jnp.concatenate([seg[:1], seg[:-1]])
    columns = [seg]
    for lag in range(1, 4):
        moved = jnp.pad(seg, (lag, 0), constant_values=-1)[:length]
        columns.append(moved == seg)
    columns.append(seg == jnp.repeat(before[::BLOCK], BLOCK))
    columns += [jnp.zeros_like(seg)] * 3
    return jnp.stack([c.astype(jnp.float32) for c in columns], axis=1)


def masks():
    shape = (BLOCK, BLOCK)
    row = lax.broadcasted_iota(jnp.int32, shape, 0)
    col = lax.broadcasted_iota(jnp.int32, shape, 1)
    return row, col


def unit_inverse(lowers):
    row, col = masks()
    out = None
    size = 0
    while (1 << size) < BLOCK:
        part = jnp.logical_and(
            (row >> (size + 1)) == (col >> (size + 1)),
            jnp.logical_and(((row >> size) & 1) == 1, ((col >> size) & 1) == 0),
        )
        cut = [jnp.where(part, low, 0.0) for low in lowers]
        if out is None:
            unit = (row == col).astype(jnp.float32)
            out = [unit - c for c in cut]
        else:
            mid = [contract(c, t, NN, True) for c, t in zip(cut, out)]
            out = [t - contract(t, m, NN, True) for t, m in zip(out, mid)]
        size += 1
    return out


def front(ext, alpha_pre, beta_pre, taps, rate, aux, key_width):
    rows = BLOCK
    wide = (rows, ext.shape[1])
    square = (BLOCK, BLOCK)
    total = spread(taps[3], wide) * lagged(ext, 0)
    for lag in range(1, 4):
        keep = jnp.broadcast_to(aux[lag], wide)
        total = total + spread(taps[3 - lag], wide) * (lagged(ext, lag) * keep)
    act = silu(total)

    def unit_rows(x):
        return x * spread(lax.rsqrt(keepsum(x * x, 1) + 1e-06), x.shape)

    return act, unit_rows


def block_terms(query, keys, beta_pre, alpha_pre, rate, aux):
    square = (BLOCK, BLOCK)
    row, col = masks()
    eye = (row == col).astype(jnp.float32)
    seg_col = jnp.broadcast_to(aux[0], square)
    seg_row = jnp.broadcast_to(jnp.sum(eye * seg_col, axis=0, keepdims=True), square)
    live = jnp.logical_and(seg_col == seg_row, row >= col)
    beta = jax.nn.sigmoid(beta_pre)
    logd = -spread(rate, alpha_pre.shape) * softplus(alpha_pre)
    incl = (row >= col).astype(jnp.float32)
    logd_row = keepsum(eye * spread(logd, square), 0)
    cum = keepsum(incl * spread(logd_row, square), 1)
    cum_row = keepsum(eye * spread(cum, square), 0)
    diff = spread(cum, square) - spread(cum_row, square)
    within = jnp.where(live, jnp.exp(jnp.where(live, diff, 0.0)), 0.0)
    carried = jnp.exp(cum) * aux[4]
    kk = mm_nt(keys, keys, True)
    strict = (row > col).astype(jnp.float32)
    lower = spread(beta, square) * within * kk * strict
    place = lax.broadcasted_iota(jnp.int32, (BLOCK, 1), 0)
    last = (place == BLOCK - 1).astype(jnp.float32)
    cum_last = spread(keepsum(cum * last, 0), cum.shape)
    seg_last = jnp.broadcast_to(jnp.sum(aux[0] * last, axis=0, keepdims=True), cum.shape)
    same = seg_last == aux[0]
    final = jnp.where(same, jnp.exp(jnp.where(same, cum_last - cum, 0.0)), 0.0)
    carried_last = keepsum(carried * last, 0)
    return beta, within, carried, lower, final, carried_last


def split_heads(ext, taps, aux, key_width):
    act, unit_rows = front(ext, None, None, taps, None, aux, key_width)
    query = unit_rows(act[:, :key_width]) * key_width ** (-0.5)
    keys = unit_rows(act[:, key_width : 2 * key_width])
    return query, keys, act[:, 2 * key_width :]


def advance(query, keys, values, terms, state, inverse, gate_out, onorm):
    beta, within, carried, lower, final, carried_last = terms
    tall = values.shape
    rhs = spread(beta, tall) * (values - spread(carried, tall) * mm_nn(keys, state))
    errs = solve(lower, rhs, inverse)
    read = spread(carried, tall) * mm_nn(query, state)
    read = read + mm_nn(within * mm_nt(query, keys), errs)
    new_state = spread(carried_last, state.shape) * state
    new_state = new_state + mm_tn(spread(final, keys.shape) * keys, errs)
    scale = lax.rsqrt(keepsum(read * read, 1) * (1.0 / tall[1]) + 1e-05)
    out = read * spread(scale, tall) * spread(onorm, tall) * silu(gate_out)
    return out, new_state


def head_inputs(h, dims, halo_ref, proj_ref, gates_ref, conv_ref, rate_ref, onorm_ref):
    heads, mix, conv, value = dims
    base = h * mix
    ext = jnp.concatenate(
        [halo_ref[:, base : base + conv], proj_ref[:, base : base + conv]], axis=0
    )
    gate_out = proj_ref[:, base + conv : base + mix]
    alpha_pre = gates_ref[:, 2 * h : 2 * h + 1]
    beta_pre = gates_ref[:, 2 * h + 1 : 2 * h + 2]
    taps = tuple(conv_ref[i : i + 1, h * conv : (h + 1) * conv] for i in range(4))
    rate = rate_ref[:, h : h + 1]
    onorm = onorm_ref[h : h + 1, :]
    return ext, gate_out, alpha_pre, beta_pre, taps, rate, onorm


def forward_kernel(dims, halo_ref, proj_ref, gates_ref, aux_ref, conv_ref, rate_ref, onorm_ref,
                   out_ref, states_ref, inv_ref, state):
    heads, mix, conv, value = dims
    key_width = (conv - value) // 2

    @pl.when(pl.program_id(1) == 0)
    def _():
        state[...] = jnp.zeros_like(state)

    aux = [aux_ref[:, i : i + 1] for i in range(5)]
    work = []
    for h in range(heads):
        ext, gate_out, alpha_pre, beta_pre, taps, rate, onorm = head_inputs(
            h, dims, halo_ref, proj_ref, gates_ref, conv_ref, rate_ref, onorm_ref
        )
        query, keys, values = split_heads(ext, taps, aux, key_width)
        terms = block_terms(query, keys, beta_pre, alpha_pre, rate, aux)
        work.append((query, keys, values, terms, gate_out, onorm))
    inverses = unit_inverse([w[3][3] for w in work])
    for h in range(heads):
        query, keys, values, terms, gate_out, onorm = work[h]
        old = state[h * key_width : (h + 1) * key_width, :]
        out, new = advance(query, keys, values, terms, old, inverses[h], gate_out, onorm)
        states_ref[0, h * key_width : (h + 1) * key_width, :] = old
        state[h * key_width : (h + 1) * key_width, :] = new
        inv_ref[0, h * BLOCK : (h + 1) * BLOCK, :] = inverses[h]
        out_ref[:, h * value : (h + 1) * value] = out.astype(out_ref.dtype)


def backward_kernel(dims, halo_ref, proj_ref, gates_ref, aux_ref, conv_ref, rate_ref, onorm_ref,
                    states_ref, inv_ref, d_out_ref,
                    d_proj_ref, d_gates_ref, d_conv_ref, d_rate_ref, d_onorm_ref, d_state, spill):
    heads, mix, conv, value = dims
    key_width = (conv - value) // 2

    @pl.when(pl.program_id(1) == 0)
    def _():
        d_state[...] = jnp.zeros_like(d_state)
        spill[...] = jnp.zeros_like(spill)

    @pl.when(jnp.logical_and(pl.program_id(0) == 0, pl.program_id(1) == 0))
    def _():
        d_conv_ref[...] = jnp.zeros_like(d_conv_ref)
        d_rate_ref[...] = jnp.zeros_like(d_rate_ref)
        d_onorm_ref[...] = jnp.zeros_like(d_onorm_ref)

    aux = [aux_ref[:, i : i + 1] for i in range(5)]
    lane = lax.broadcasted_iota(jnp.int32, (BLOCK, 2 * heads), 1)
    d_gates = jnp.zeros((BLOCK, 2 * heads), jnp.float32)
    for h in range(heads):
        ext, gate_out, alpha_pre, beta_pre, taps, rate, onorm = head_inputs(
            h, dims, halo_ref, proj_ref, gates_ref, conv_ref, rate_ref, onorm_ref
        )
        old = states_ref[0, h * key_width : (h + 1) * key_width, :]
        inverse = inv_ref[0, h * BLOCK : (h + 1) * BLOCK, :]

        act, act_back = jax.vjp(
            lambda e, t: front(e, None, None, t, None, aux, key_width)[0], ext, taps
        )
        raw_q = act[:, :key_width]
        raw_k = act[:, key_width : 2 * key_width]
        values = act[:, 2 * key_width :]

        def rest(raw_q, raw_k, values, gate_out, alpha_pre, beta_pre, rate, onorm, old):
            def unit_rows(x):
                return x * spread(lax.rsqrt(keepsum(x * x, 1) + 1e-06), x.shape)

            query = unit_rows(raw_q) * key_width ** (-0.5)
            keys = unit_rows(raw_k)
            terms = block_terms(query, keys, beta_pre, alpha_pre, rate, aux)
            return advance(query, keys, values, terms, old, inverse, gate_out, onorm)

        _, back = jax.vjp(
            rest, raw_q, raw_k, values, gate_out, alpha_pre, beta_pre, rate, onorm, old
        )
        d_out = d_out_ref[:, h * value : (h + 1) * value]
        span = slice(h * key_width, (h + 1) * key_width)
        d_q, d_k, d_v, d_gate, d_alpha, d_beta, d_rate, d_onorm, d_old = back(
            (d_out, d_state[span, :])
        )
        d_state[span, :] = d_old
        d_ext, d_taps = act_back(jnp.concatenate([d_q, d_k, d_v], axis=1))
        cols = slice(h * conv, (h + 1) * conv)
        carry = jnp.concatenate(
            [jnp.zeros((BLOCK - HALO, conv), jnp.float32), spill[:, cols]], axis=0
        )
        d_mixed = d_ext[HALO:] + carry
        spill[:, cols] = d_ext[:HALO]
        base = h * mix
        d_proj_ref[:, base : base + conv] = d_mixed.astype(d_proj_ref.dtype)
        d_proj_ref[:, base + conv : base + mix] = d_gate.astype(d_proj_ref.dtype)
        for i in range(4):
            d_conv_ref[i : i + 1, cols] += d_taps[i]
        d_rate_ref[h : h + 1, :] += jnp.broadcast_to(d_rate, (1, 128))
        d_onorm_ref[h : h + 1, :] += d_onorm
        d_gates = d_gates + jnp.where(lane == 2 * h, jnp.broadcast_to(d_alpha, lane.shape), 0.0)
        d_gates = d_gates + jnp.where(lane == 2 * h + 1, jnp.broadcast_to(d_beta, lane.shape), 0.0)
    d_gates_ref[...] = d_gates.astype(d_gates_ref.dtype)


def common_specs(dims, blocks, order):
    heads, mix, conv, value = dims
    ratio = BLOCK // HALO
    at = lambda s, b: s * blocks + order(b)
    return [
        pl.BlockSpec((HALO, heads * mix), lambda s, b: (jnp.maximum(at(s, b) * ratio - 1, 0), 0)),
        pl.BlockSpec((BLOCK, heads * mix), lambda s, b: (at(s, b), 0)),
        pl.BlockSpec((BLOCK, heads * 2), lambda s, b: (at(s, b), 0)),
        pl.BlockSpec((BLOCK, 8), lambda s, b: (at(s, b), 0)),
        pl.BlockSpec((4, heads * conv), lambda s, b: (0, 0)),
        pl.BlockSpec((1, heads), lambda s, b: (0, 0)),
        pl.BlockSpec((heads, value), lambda s, b: (0, 0)),
    ], at


def mixer_forward(proj, gates_pre, aux, conv2d, rate, onorm, dims, seqs, interpret=False):
    heads, mix, conv, value = dims
    key_width = (conv - value) // 2
    rows = proj.shape[0]
    blocks = rows // seqs // BLOCK
    specs, at = common_specs(dims, blocks, lambda b: b)
    return pl.pallas_call(
        functools.partial(forward_kernel, dims),
        grid=(seqs, blocks),
        in_specs=specs,
        out_specs=[
            pl.BlockSpec((BLOCK, heads * value), lambda s, b: (at(s, b), 0)),
            pl.BlockSpec((1, heads * key_width, value), lambda s, b: (at(s, b), 0, 0)),
            pl.BlockSpec((1, heads * BLOCK, BLOCK), lambda s, b: (at(s, b), 0, 0)),
        ],
        out_shape=[
            jax.ShapeDtypeStruct((rows, heads * value), jnp.bfloat16),
            jax.ShapeDtypeStruct((seqs * blocks, heads * key_width, value), jnp.float32),
            jax.ShapeDtypeStruct((seqs * blocks, heads * BLOCK, BLOCK), jnp.float32),
        ],
        scratch_shapes=[pltpu.VMEM((heads * key_width, value), jnp.float32)],
        cost_estimate=pl.CostEstimate(flops=rows * heads * 2000000, bytes_accessed=rows * heads * 8192, transcendentals=0),
        name="mixer_forward",
        interpret=interpret,
    )(proj, proj, gates_pre, aux, conv2d, rate, onorm)


def mixer_backward(proj, gates_pre, aux, conv2d, rate, onorm, states, inverses, d_heads, dims, seqs, interpret=False):
    heads, mix, conv, value = dims
    key_width = (conv - value) // 2
    rows = proj.shape[0]
    blocks = rows // seqs // BLOCK
    specs, at = common_specs(dims, blocks, lambda b: blocks - 1 - b)
    return pl.pallas_call(
        functools.partial(backward_kernel, dims),
        grid=(seqs, blocks),
        in_specs=specs + [
            pl.BlockSpec((1, heads * key_width, value), lambda s, b: (at(s, b), 0, 0)),
            pl.BlockSpec((1, heads * BLOCK, BLOCK), lambda s, b: (at(s, b), 0, 0)),
            pl.BlockSpec((BLOCK, heads * value), lambda s, b: (at(s, b), 0)),
        ],
        out_specs=[
            pl.BlockSpec((BLOCK, heads * mix), lambda s, b: (at(s, b), 0)),
            pl.BlockSpec((BLOCK, heads * 2), lambda s, b: (at(s, b), 0)),
            pl.BlockSpec((4, heads * conv), lambda s, b: (0, 0)),
            pl.BlockSpec((heads, 128), lambda s, b: (0, 0)),
            pl.BlockSpec((heads, value), lambda s, b: (0, 0)),
        ],
        out_shape=[
            jax.ShapeDtypeStruct((rows, heads * mix), jnp.bfloat16),
            jax.ShapeDtypeStruct((rows, heads * 2), jnp.bfloat16),
            jax.ShapeDtypeStruct((4, heads * conv), jnp.float32),
            jax.ShapeDtypeStruct((heads, 128), jnp.float32),
            jax.ShapeDtypeStruct((heads, value), jnp.float32),
        ],
        scratch_shapes=[
            pltpu.VMEM((heads * key_width, value), jnp.float32),
            pltpu.VMEM((HALO, heads * conv), jnp.float32),
        ],
        cost_estimate=pl.CostEstimate(flops=rows * heads * 5000000, bytes_accessed=rows * heads * 12288, transcendentals=0),
        name="mixer_backward",
        interpret=interpret,
    )(proj, proj, gates_pre, aux, conv2d, rate, onorm, states, inverses, d_heads)


def swish_gate(gate, up):
    return jax.nn.silu(gate) * up


def local(
    tokens,
    seg_starts,
    norm1_gain,
    w_mix,
    w_gates,
    conv_w,
    decay_rate,
    onorm_gain,
    w_out,
    norm2_gain,
    w_gu,
    w_down,
    cotangent,
):
    f32 = jnp.float32
    bf16 = jnp.bfloat16
    local_rows, width = tokens.shape
    seqs = seg_starts.shape[0]
    heads = w_mix.shape[1]
    mix_cols = w_mix.shape[2]
    value_width = onorm_gain.shape[1]
    hidden = w_down.shape[0]
    mix2d = w_mix.reshape(width, heads * mix_cols)
    gates2d = w_gates.reshape(width, heads * 2)
    out2d = w_out.reshape(heads * value_width, width)
    gu2d = w_gu.reshape(width, 2 * hidden)
    resid = tokens.astype(f32)
    normed1 = rms_norm(resid, norm1_gain).astype(bf16)
    rows1 = lax.all_gather(normed1, "tensor", axis=0, tiled=True)
    total_rows = rows1.shape[0]
    length = total_rows // seqs
    dims = (heads, mix_cols, conv_w.shape[2], value_width)
    proj = jnp.dot(rows1, mix2d, preferred_element_type=f32)
    gates_pre = jnp.dot(rows1, gates2d, preferred_element_type=f32)
    aux = jax.vmap(segment_ids, in_axes=(0, None))(seg_starts, length).reshape(total_rows, 8)
    mixer_args = (proj, gates_pre, aux, conv_w.reshape(4, -1), decay_rate[None, :], onorm_gain)
    mixed, states, inverses = mixer_forward(*mixer_args, dims, seqs)
    cot_rows = lax.all_gather(cotangent, "tensor", axis=0, tiled=True)
    mixed, cot_rows = lax.optimization_barrier((mixed, cot_rows))
    resid2 = resid + lax.psum_scatter(
        jnp.dot(mixed, out2d, preferred_element_type=f32).astype(jnp.bfloat16),
        "tensor",
        scatter_dimension=0,
        tiled=True,
    ).astype(jnp.float32)
    normed2 = rms_norm(resid2, norm2_gain).astype(bf16)
    rows2 = lax.all_gather(normed2, "tensor", axis=0, tiled=True)
    gu = jnp.dot(rows2, gu2d, preferred_element_type=f32).reshape(total_rows, 2, hidden)
    act = swish_gate(gu[:, 0], gu[:, 1]).astype(bf16)
    ffn_part = jnp.dot(act, w_down, preferred_element_type=f32).astype(bf16)
    grad_down = jnp.dot(cot_rows.T, act, preferred_element_type=f32).astype(bf16)
    d_act = jnp.dot(cot_rows, w_down.T, preferred_element_type=f32)
    _, swish_back = jax.vjp(swish_gate, gu[:, 0], gu[:, 1])
    d_gate, d_up = swish_back(d_act)
    d_gu = jnp.stack([d_gate, d_up], axis=1).astype(bf16).reshape(total_rows, 2 * hidden)
    grad_gu = jnp.dot(rows2.T, d_gu, preferred_element_type=f32).astype(bf16)
    d_normed2 = lax.psum_scatter(
        jnp.dot(d_gu, gu2d.T, preferred_element_type=f32).astype(jnp.bfloat16),
        "tensor",
        scatter_dimension=0,
        tiled=True,
    ).astype(jnp.float32)
    _, norm2_back = jax.vjp(rms_norm, resid2, norm2_gain)
    d_resid_ffn, gain2_part = norm2_back(d_normed2)
    d_resid2 = cotangent.astype(f32) + d_resid_ffn
    d_rows = lax.all_gather(d_resid2.astype(bf16), "tensor", axis=0, tiled=True)
    grad_out = jnp.dot(d_rows.T, mixed, preferred_element_type=f32).astype(bf16)
    d_heads = jnp.dot(d_rows, out2d.T, preferred_element_type=f32)
    d_heads, ffn_part = lax.optimization_barrier((d_heads, ffn_part))
    ffn_sum = lax.psum_scatter(ffn_part, "tensor", scatter_dimension=0, tiled=True)
    d_proj_b, d_gates_b, d_conv, d_rate, d_onorm = mixer_backward(
        *mixer_args, states, inverses, d_heads, dims, seqs
    )
    d_proj_b, ffn_sum = lax.optimization_barrier((d_proj_b, ffn_sum))
    output = (resid2 + ffn_sum.astype(f32)).astype(bf16)
    d_conv = d_conv.reshape(conv_w.shape)
    d_rate = d_rate[:, 0]
    grad_mix = jnp.dot(rows1.T, d_proj_b, preferred_element_type=f32).astype(bf16)
    grad_gates = jnp.dot(rows1.T, d_gates_b, preferred_element_type=f32).astype(bf16)
    d_normed1 = lax.psum_scatter(
        (
            jnp.dot(d_proj_b, mix2d.T, preferred_element_type=f32)
            + jnp.dot(d_gates_b, gates2d.T, preferred_element_type=f32)
        ).astype(jnp.bfloat16),
        "tensor",
        scatter_dimension=0,
        tiled=True,
    ).astype(jnp.float32)
    pad = -(2 * heads) % 128
    grads = jnp.concatenate(
        [grad_mix, grad_gu, grad_down, grad_out, jnp.pad(grad_gates, ((0, 0), (0, pad)))], axis=1
    )
    d_normed1, grads = lax.optimization_barrier((d_normed1, grads))
    _, norm1_back = jax.vjp(rms_norm, resid, norm1_gain)
    d_resid1, gain1_part = norm1_back(d_normed1)
    grad_tokens = (d_resid2 + d_resid1).astype(bf16)
    grad_conv, grad_rate, grad_onorm = lax.psum((d_conv, d_rate, d_onorm), "dp")
    shares = lax.psum_scatter(grads, "dp", scatter_dimension=0, tiled=True).astype(f32)
    cuts = []
    place = 0
    for size in (heads * mix_cols, 2 * hidden, hidden, heads * value_width, 2 * heads):
        cuts.append(shares[:, place : place + size])
        place += size
    mix_share = cuts[0].reshape(-1, heads, mix_cols)
    gu_share = cuts[1].reshape(-1, 2, hidden)
    down_share = cuts[2].T
    out_share = cuts[3].T.reshape(heads, value_width, -1)
    gates_share = cuts[4].reshape(-1, heads, 2)
    gain1_share = lax.psum_scatter(gain1_part, "dp", scatter_dimension=0, tiled=True)
    gain2_share = lax.psum_scatter(gain2_part, "dp", scatter_dimension=0, tiled=True)
    gain1_total, gain2_total = lax.psum((gain1_share, gain2_share), "tensor")
    return (
        output,
        grad_tokens,
        gain1_total,
        mix_share,
        gates_share,
        grad_conv,
        grad_rate,
        grad_onorm,
        out_share,
        gain2_total,
        gu_share,
        down_share,
    )


def solution(mesh):
    in_specs = (
        P(("dp", "tensor"), None),
        P("dp", None),
        P(),
        P(None, "tensor", None),
        P(None, "tensor", None),
        P(None, "tensor", None),
        P("tensor"),
        P("tensor", None),
        P("tensor", None, None),
        P(),
        P(None, None, "tensor"),
        P("tensor", None),
        P(("dp", "tensor"), None),
    )
    out_specs = (
        P(("dp", "tensor"), None),
        P(("dp", "tensor"), None),
        P("dp"),
        P("dp", "tensor", None),
        P("dp", "tensor", None),
        P(None, "tensor", None),
        P("tensor"),
        P("tensor", None),
        P("tensor", None, "dp"),
        P("dp"),
        P("dp", None, "tensor"),
        P("tensor", "dp"),
    )
    return jax.shard_map(local, mesh=mesh, in_specs=in_specs, out_specs=out_specs, check_vma=False)
```

profile of v0, /device:TPU:0, one launch (start us, length us, event | category | flops | bytes accessed | tf_op | source)
XLA Modules:
  0.0 406.0 jit_solution(492660269775440285)
XLA Ops:
  7.2 1.2 fusion.18
  8.5 1.8 fusion.11
  10.4 0.7 all-gather.7.cloned.1.call-update
  11.1 0.7 fusion.20
  11.9 0.3 reduce-window.6
  12.2 0.2 slice_reduce_fusion
  12.4 0.2 reduce-window.9
  12.6 0.5 slice.69
  13.2 0.7 pad_add_fusion
  14.1 0.7 reshape.267
  14.8 1.3 copy.84
  16.3 0.8 copy.69
  17.2 4.1 %copy.83 = bf16[128,8,2,768]{3,1,2,0:T(8,128)(2,1)} copy(bf16[128,8,2,768]{3,2,1,0:T(2,128)(2,1)} %bitcast.95) | data formatting | bytes 6291456
  21.3 8.6 %all-gather.5.cloned.1.call-done = bf16[512,1024]{1,0:T(8,128)(2,1)} async-done(((bf16[128,1024]{1,0:T(8,128)(2,1)}), bf16[512,1024]{1,0:T(8,128)(2,1)}) %all-gather.5.cloned.1.call-update) | async-done | bytes 1048592 | tf_op jit(solution)/shard_map/all_gather | solution.py:467
  29.9 2.3 fusion.28.gates_ref
  32.2 5.7 %fusion.27.halo_ref.proj_ref = f32[512,1536]{1,0:T(8,128)} fusion(bf16[512,1024]{1,0:T(8,128)(2,1)} %all-gather.5.cloned.1.call-done, bf16[1024,1536]{1,0:T(8,128)(2,1)} %bitcast.96), kind=kOutput, calls=%fused_computation.75 | convolution fusion | flops 1610612736 | bytes 7340032 | tf_op jit(solution)/shard_map/dot_general | solution.py:471
  37.9 24.9 %mixer_forward.1 = (bf16[512,512]{1,0:T(8,128)(2,1)}, f32[8,256,256]{2,1,0:T(8,128)}, f32[8,128,64]{2,1,0:T(8,128)}) custom-call(f32[512,1536]{1,0:T(8,128)} %fusion.27.halo_ref.proj_ref, f32[512,1536]{1,0:T(8,128)} %fusion.27.halo_ref.proj_ref, f32[512,4]{1,0:T(8,128)} %fusion.28.gates_ref, f32[512,8]{1,0:T(8,128)} %bitcast.100, f32[4,1024]{1,0:T(4,128)} %bitcast.111, ...), custom_call_target="tpu_custom_call" | custom-call | flops 2048000000 | bytes 8388608 | tf_op jit(solution)/shard_map/mixer_forward/pallas_call | solution.py:375
  62.9 3.2 convolution_convert_fusion.5
  66.1 24.9 %reduce-scatter.6.cloned.1.call-done = bf16[128,1024]{1,0:T(8,128)(2,1)} async-done(((bf16[512,1024]{1,0:T(8,128)(2,1)}), bf16[128,1024]{1,0:T(8,128)(2,1)}) %reduce-scatter.6.cloned.1.call-update) | async-done | bytes 262160 | tf_op jit(solution)/shard_map/reduce_scatter | solution.py:478
  91.1 1.1 multiply_reduce_fusion
  92.2 1.8 multiply_convert_fusion.1
  94.0 16.8 %all-gather.9.cloned.1.call-done = bf16[512,1024]{1,0:T(8,128)(2,1)} async-done(((bf16[128,1024]{1,0:T(8,128)(2,1)}), bf16[512,1024]{1,0:T(8,128)(2,1)}) %all-gather.9.cloned.1.call-update) | async-done | bytes 1048592 | tf_op jit(solution)/shard_map/all_gather | solution.py:485
  110.9 3.1 fusion
  114.0 1.5 fusion.4
  115.6 0.9 copy-done.12
  116.4 0.2 copy-done.14
  116.7 2.8 bitcast_convert_fusion
  119.6 24.9 %reduce-scatter.8.cloned.1.call-done = bf16[128,1024]{1,0:T(8,128)(2,1)} async-done(((bf16[512,1024]{1,0:T(8,128)(2,1)}), bf16[128,1024]{1,0:T(8,128)(2,1)}) %reduce-scatter.8.cloned.1.call-update) | async-done | bytes 262160 | tf_op jit(solution)/shard_map/reduce_scatter | solution.py:495
  144.5 1.2 fusion.14
  145.7 2.0 fusion.26
  147.7 0.2 reduce-scatter.10.cloned.1.call-start
  147.9 0.4 multiply_convert_fusion
  148.4 0.8 copy-done.10
  149.3 2.0 convolution_convert_fusion.3
  151.3 13.2 %all-gather.11.cloned.1.call-done = bf16[512,1024]{1,0:T(8,128)(2,1)} async-done(((bf16[128,1024]{1,0:T(8,128)(2,1)}), bf16[512,1024]{1,0:T(8,128)(2,1)}) %all-gather.11.cloned.1.call-update) | async-done | bytes 1048592 | tf_op jit(solution)/shard_map/all_gather | solution.py:504
  164.5 2.9 fusion.29.d_out_ref
  167.5 26.9 %mixer_backward.1 = (bf16[512,1536]{1,0:T(8,128)(2,1)}, bf16[512,4]{1,0:T(8,128)(2,1)}, f32[4,1024]{1,0:T(4,128)}, f32[2,128]{1,0:T(2,128)}, f32[2,256]{1,0:T(2,128)}) custom-call(f32[512,1536]{1,0:T(8,128)} %fusion.27.halo_ref.proj_ref, f32[512,1536]{1,0:T(8,128)} %fusion.27.halo_ref.proj_ref, f32[512,4]{1,0:T(8,128)} %fusion.28.gates_ref, ...), custom_call_target="tpu_custom_call" | custom-call | flops 5120000000 | bytes 12582912 | tf_op jit(solution)/shard_map/mixer_backward/pallas_call | solution.py:402
  194.5 4.2 %fusion.30 = f32[512,1024]{1,0:T(8,128)S(1)} fusion(bf16[512,1536]{1,0:T(8,128)(2,1)} %get-tuple-element.37, bf16[1024,1536]{1,0:T(8,128)(2,1)} %bitcast.97), kind=kOutput, calls=%fused_computation.78 | convolution fusion | flops 1610612736 | bytes 6815744 | tf_op jit(solution)/shard_map/dot_general | solution.py:520
  198.8 1.4 add_convert_fusion
  200.2 3.2 convolution_convert_fusion.2
  203.5 1.8 copy.73
  205.3 1.3 maximum_convert_fusion
  206.7 3.4 convolution_convert_fusion
  210.2 0.3 convolution_convert_fusion.6
  210.4 0.9 copy.82
  211.3 1.0 pad.19.clone
  212.3 3.2 convolution_convert_fusion.4
  215.6 3.5 convolution_convert_fusion.1
  219.0 13.7 %concatenate.7 = bf16[1024,4288]{1,0:T(8,128)(2,1)} concatenate(bf16[1024,1536]{1,0:T(8,128)(2,1)} %convolution_convert_fusion.1, bf16[1024,1408]{1,0:T(8,128)(2,1)} %convolution_convert_fusion, bf16[1024,704]{1,0:T(8,128)(2,1)S(1)} %copy.73, bf16[1024,512]{1,0:T(8,128)(2,1)} %convolution_convert_fusion.4, bf16[1024,128]{1,0:T(8,128)(2,1)S(1)} %pad.19.clone), dimensions={1} | concatenate | bytes 17563648 | tf_op jit(solution)/shard_map/concatenate | solution.py:528
  232.8 1.0 convert_element_type.136
  234.0 0.5 copy-done.35
  234.4 0.6 dynamic-slice
  235.9 0.2 fusion.12
  236.1 40.0 %all-reduce.6 = (f32[1024]{0:T(1024)S(1)}, f32[4,2,512]{2,1,0:T(2,128)}, f32[2]{0:T(128)}, f32[2,256]{1,0:T(2,128)}, f32[1024]{0:T(1024)S(1)}) all-reduce(f32[1024]{0:T(1024)S(1)} %get-tuple-element.106, f32[4,2,512]{2,1,0:T(2,128)S(1)} %reshape.280, f32[2]{0:T(128)S(1)} %slice_reduce_fusion.1, ...), channel_id=6, replica_groups=mesh['dp'=8,'tensor'=4] {'dp'}, use_global_device_ids=true, to_apply=%region_12.13.clone | all-reduce | flops 6658 | bytes 53264
  276.2 6.5 %all-reduce.7 = (f32[128]{0:T(128)}, f32[128]{0:T(128)}) all-reduce(f32[128]{0:T(128)S(1)} %dynamic-slice.1, f32[128]{0:T(128)S(1)} %dynamic-slice.3), channel_id=1, replica_groups=mesh['dp'=8,'tensor'=4] {'tensor'}, use_global_device_ids=true, to_apply=%region_13.14 | all-reduce | flops 256 | bytes 2048 | tf_op jit(solution)/shard_map/psum | solution.py:549
  282.8 1.2 fusion.17
  284.0 105.5 %reduce-scatter.14.cloned.1.call-done = bf16[128,4288]{1,0:T(8,128)(2,1)} async-done(((bf16[1024,4288]{1,0:T(8,128)(2,1)}), bf16[128,4288]{1,0:T(8,128)(2,1)}) %reduce-scatter.14.cloned.1.call-update) | async-done | bytes 1097744 | tf_op jit(solution)/shard_map/reduce_scatter | solution.py:536
  389.5 1.5 convert_element_type.144
  391.3 0.7 copy.75
  392.0 1.1 copy.76
  393.1 2.1 slice.73
  395.2 2.5 reshape.278
  397.8 0.9 copy.78
  398.7 0.8 copy.81
  (114 shorter events, 2.0 us)
Async XLA Ops:
  7.2 103.7 %copy-start = (bf16[1024,2,704]{0,2,1:T(8,128)(2,1)S(1)}, bf16[1024,2,704]{0,2,1:T(8,128)(2,1)}, u32[]{:S(2)}) copy-start(bf16[1024,2,704]{0,2,1:T(8,128)(2,1)} %param.23) | copy-start | bytes 8650756
  7.2 22.7 %all-gather.5.cloned.1.call-start = ((), (), s32[]{:S(2)}) async-start(), calls=%async_computation.5 | async-start | bytes 1310720 | tf_op jit(solution)/shard_map/all_gather | solution.py:467
  8.5 2.6 copy-start.27
  8.5 3.4 copy-start.22
  10.3 52.5 %all-gather.7.cloned.1.call-start = ((), (), s32[]{:S(2)}) async-start(), calls=%async_computation.6 | async-start | bytes 1310720 | tf_op jit(solution)/shard_map/all_gather | solution.py:476
  11.1 80.0 %reduce-scatter.6.cloned.1.call-start = ((), (), s32[]{:S(2)}) async-start(), calls=%async_computation.7 | async-start | bytes 1310720 | tf_op jit(solution)/shard_map/reduce_scatter | solution.py:478
  62.9 28.2 %copy-start.2 = (bf16[128,1024]{1,0:T(8,128)(2,1)S(1)}, bf16[128,1024]{1,0:T(8,128)(2,1)}, u32[]{:S(2)}) copy-start(bf16[128,1024]{1,0:T(8,128)(2,1)} %param.13) | copy-start | bytes 786436
  62.9 29.3 %copy-start.17 = (f32[1024]{0:T(1024)S(1)}, f32[1024]{0:T(1024)}, u32[]{:S(2)}) copy-start(f32[1024]{0:T(1024)} %param.22) | copy-start | bytes 12292
  66.1 44.8 %all-gather.9.cloned.1.call-start = ((), (), s32[]{:S(2)}) async-start(), calls=%async_computation.8 | async-start | bytes 1310720 | tf_op jit(solution)/shard_map/all_gather | solution.py:485
  92.2 53.5 %copy-start.20 = (f32[128]{0:T(128)}, f32[128]{0:T(128)S(1)}, u32[]{:S(2)}) copy-start(f32[128]{0:T(128)S(1)} %fusion.25) | copy-start | bytes 1540
  94.0 50.5 %reduce-scatter.8.cloned.1.call-start = ((), (), s32[]{:S(2)}) async-start(), calls=%async_computation.9 | async-start | bytes 1310720 | tf_op jit(solution)/shard_map/reduce_scatter | solution.py:495
  110.8 3.1 copy-start.29
  110.9 3.1 copy-start.32
  114.0 1.6 copy-start.6
  115.6 0.9 copy-start.12
  115.6 1.1 copy-start.14
  116.7 27.8 %copy-start.3 = (bf16[128,1024]{1,0:T(8,128)(2,1)S(1)}, bf16[128,1024]{1,0:T(8,128)(2,1)}, u32[]{:S(2)}) copy-start(bf16[128,1024]{1,0:T(8,128)(2,1)} %reduce-scatter.6.cloned.1.call-done) | copy-start | bytes 786436
  119.5 28.4 %copy-start.7 = (f32[512,2,704]{0,2,1:T(8,128)S(1)}, f32[512,2,704]{0,2,1:T(8,128)}, u32[]{:S(2)}) copy-start(f32[512,2,704]{0,2,1:T(8,128)} %copy-done.6) | copy-start | bytes 8650756
  119.5 45.0 %all-gather.11.cloned.1.call-start = ((), (), s32[]{:S(2)}) async-start(), calls=%async_computation.10 | async-start | bytes 1310720 | tf_op jit(solution)/shard_map/all_gather | solution.py:504
  145.7 2.7 copy-start.25
  147.7 46.8 %reduce-scatter.10.cloned.1.call-start = ((), (), s32[]{:S(2)}) async-start(), calls=%async_computation.11 | async-start | bytes 1310720 | tf_op jit(solution)/shard_map/reduce_scatter | solution.py:508
  147.9 1.4 copy-start.30
  148.4 0.9 copy-start.10
  149.3 15.3 %copy-start.31 = (bf16[2,256,1024]{2,1,0:T(8,128)(2,1)S(1)}, bf16[2,256,1024]{2,1,0:T(8,128)(2,1)}, u32[]{:S(2)}) copy-start(bf16[2,256,1024]{2,1,0:T(8,128)(2,1)} %param.21) | copy-start | bytes 3145732
  167.5 65.3 %reduce-scatter.12.cloned.1.call-start = ((), (), s32[]{:S(2)}) async-start(), calls=%async_computation.12 | async-start | bytes 1310720 | tf_op jit(solution)/shard_map/reduce_scatter | solution.py:518
  194.5 4.2 %copy-start.15 = (bf16[512,4]{1,0:T(8,128)(2,1)S(1)}, bf16[512,4]{1,0:T(8,128)(2,1)}, u32[]{:S(2)}) copy-start(bf16[512,4]{1,0:T(8,128)(2,1)} %get-tuple-element.38) | copy-start | bytes 12292
  198.7 1.5 copy-start.11
  200.2 189.4 %reduce-scatter.14.cloned.1.call-start = ((), (), s32[]{:S(2)}) async-start(), calls=%async_computation.13 | async-start | bytes 10027008 | tf_op jit(solution)/shard_map/reduce_scatter | solution.py:536
  203.5 1.8 copy-start.13
  205.2 1.5 copy-start.33
  206.7 3.4 copy-start.5
  212.3 3.2 copy-start.36
  233.8 0.7 copy-start.35
  233.8 1.9 copy-start.19
  233.8 1.9 copy-start.34
  233.8 2.0 copy-start.18
  233.8 2.0 copy-start.23
  233.9 2.2 copy-start.24
  233.9 48.9 %copy-start.28 = (f32[128]{0:T(128)S(1)}, f32[128]{0:T(128)}, u32[]{:S(2)}) copy-start(f32[128]{0:T(128)} %copy-done.27) | copy-start | bytes 1540
  233.9 48.9 %copy-start.8 = (bf16[128,1024]{1,0:T(8,128)(2,1)S(1)}, bf16[128,1024]{1,0:T(8,128)(2,1)}, u32[]{:S(2)}) copy-start(bf16[128,1024]{1,0:T(8,128)(2,1)} %param.25) | copy-start | bytes 786436
  233.9 48.9 %copy-start.9 = (bf16[128,1024]{1,0:T(8,128)(2,1)S(1)}, bf16[128,1024]{1,0:T(8,128)(2,1)}, u32[]{:S(2)}) copy-start(bf16[128,1024]{1,0:T(8,128)(2,1)} %reduce-scatter.8.cloned.1.call-done) | copy-start | bytes 786436
  233.9 48.9 %copy-start.16 = (bf16[128,1024]{1,0:T(8,128)(2,1)S(1)}, bf16[128,1024]{1,0:T(8,128)(2,1)}, u32[]{:S(2)}) copy-start(bf16[128,1024]{1,0:T(8,128)(2,1)} %reduce-scatter.10.cloned.1.call-done) | copy-start | bytes 786436
  233.9 48.9 %copy-start.21 = (f32[128]{0:T(128)S(1)}, f32[128]{0:T(128)}, u32[]{:S(2)}) copy-start(f32[128]{0:T(128)} %copy-done.20) | copy-start | bytes 1540
  233.9 48.9 %copy-start.26 = (f32[128]{0:T(128)S(1)}, f32[128]{0:T(128)}, u32[]{:S(2)}) copy-start(f32[128]{0:T(128)} %copy-done.25) | copy-start | bytes 1540
  389.5 1.7 copy-start.4
  393.1 6.4 %copy-start.1 = (bf16[1024,2,704]{0,2,1:T(8,128)(2,1)S(1)}, bf16[1024,2,704]{0,2,1:T(8,128)(2,1)}, u32[]{:S(2)}) copy-start(bf16[1024,2,704]{0,2,1:T(8,128)(2,1)} %param.23) | copy-start | bytes 8650756
Sparse Core Ops, SparseCore 0:
  10.4 19.4 all-gather.4
  31.5 16.6 all-gather.6
  66.2 24.8 reduce-scatter.5
  94.1 16.6 all-gather.8
  119.6 24.7 reduce-scatter.7
  147.8 16.6 all-gather.10
  167.6 24.7 reduce-scatter.9
  200.3 24.7 reduce-scatter.11
  234.1 155.4 reduce-scatter.13
where the time goes:
time: 407 us; the launch traced here: 406 us
  waiting for transfers between devices  195 us (48%)
  Pallas kernels  51.8 us (13%)
  blocking collectives  46.6 us (11%)
  matrix products  42.8 us (11%)
  local copies, waits for them, and re-layouts  37.7 us (9%)
  other arithmetic  16.8 us (4%)
  between operations  15 us (4%)
    reduce_scatter x1, waiting for transfers between devices, local(): lax.psum_scatter(grads, 'dp', scatter_dimension=0, tiled=True).astype(f32)  106 us
    unnamed x1, blocking collectives  40 us
    pallas_call x1, Pallas kernels, mixer_backward(): pl.pallas_call(functools.partial(backward_kernel, dims), grid=(seqs, bloc...  26.9 us
    reduce_scatter x1, waiting for transfers between devices, local(): lax.psum_scatter(jnp.dot(mixed, out2d, preferred_element_type=f32).astype...  24.9 us
    pallas_call x1, Pallas kernels, mixer_forward(): pl.pallas_call(functools.partial(forward_kernel, dims), grid=(seqs, block...  24.9 us
    reduce_scatter x1, waiting for transfers between devices, local(): lax.psum_scatter(jnp.dot(d_gu, gu2d.T, preferred_element_type=f32).astype...  24.9 us
    all_gather x1, waiting for transfers between devices, local(): rows2 = lax.all_gather(normed2, 'tensor', axis=0, tiled=True)  16.8 us
    concatenate x1, local copies, waits for them, and re-layouts, local(): jnp.concatenate([grad_mix, grad_gu, grad_down, grad_out, jnp.pad(grad_gat...  13.7 us
  transfers between devices with their start and end apart: 9, of which 6 were waited for; matrix products, arithmetic and copies ran while one was open for 14% of the time, Pallas kernels for 13%

commit v1 on v0

--- a/solution.py
+++ b/solution.py
@@ -9,6 +9,9 @@
 
 BLOCK = 64
 HALO = 8
+LANES = 128
+MESH = pl.DeviceIdType.MESH
+VMEM = pl.BlockSpec(memory_space=pltpu.VMEM)
 HI = lax.Precision.HIGHEST
 
 
@@ -298,8 +301,8 @@
         d_onorm_ref[...] = jnp.zeros_like(d_onorm_ref)
 
     aux = [aux_ref[:, i : i + 1] for i in range(5)]
-    lane = lax.broadcasted_iota(jnp.int32, (BLOCK, 2 * heads), 1)
-    d_gates = jnp.zeros((BLOCK, 2 * heads), jnp.float32)
+    lane = lax.broadcasted_iota(jnp.int32, (BLOCK, LANES), 1)
+    d_gates = jnp.zeros((BLOCK, LANES), jnp.float32)
     for h in range(heads):
         ext, gate_out, alpha_pre, beta_pre, taps, rate, onorm = head_inputs(
             h, dims, halo_ref, proj_ref, gates_ref, conv_ref, rate_ref, onorm_ref
@@ -358,7 +361,7 @@
     return [
         pl.BlockSpec((HALO, heads * mix), lambda s, b: (jnp.maximum(at(s, b) * ratio - 1, 0), 0)),
         pl.BlockSpec((BLOCK, heads * mix), lambda s, b: (at(s, b), 0)),
-        pl.BlockSpec((BLOCK, heads * 2), lambda s, b: (at(s, b), 0)),
+        pl.BlockSpec((BLOCK, LANES), lambda s, b: (at(s, b), 0)),
         pl.BlockSpec((BLOCK, 8), lambda s, b: (at(s, b), 0)),
         pl.BlockSpec((4, heads * conv), lambda s, b: (0, 0)),
         pl.BlockSpec((1, heads), lambda s, b: (0, 0)),
@@ -409,14 +412,14 @@
         ],
         out_specs=[
             pl.BlockSpec((BLOCK, heads * mix), lambda s, b: (at(s, b), 0)),
-            pl.BlockSpec((BLOCK, heads * 2), lambda s, b: (at(s, b), 0)),
+            pl.BlockSpec((BLOCK, LANES), lambda s, b: (at(s, b), 0)),
             pl.BlockSpec((4, heads * conv), lambda s, b: (0, 0)),
             pl.BlockSpec((heads, 128), lambda s, b: (0, 0)),
             pl.BlockSpec((heads, value), lambda s, b: (0, 0)),
         ],
         out_shape=[
             jax.ShapeDtypeStruct((rows, heads * mix), jnp.bfloat16),
-            jax.ShapeDtypeStruct((rows, heads * 2), jnp.bfloat16),
+            jax.ShapeDtypeStruct((rows, LANES), jnp.bfloat16),
             jax.ShapeDtypeStruct((4, heads * conv), jnp.float32),
             jax.ShapeDtypeStruct((heads, 128), jnp.float32),
             jax.ShapeDtypeStruct((heads, value), jnp.float32),
@@ -431,135 +434,523 @@
     )(proj, proj, gates_pre, aux, conv2d, rate, onorm, states, inverses, d_heads)
 
 
-def swish_gate(gate, up):
-    return jax.nn.silu(gate) * up
-
-
-def local(
-    tokens,
-    seg_starts,
-    norm1_gain,
-    w_mix,
-    w_gates,
-    conv_w,
-    decay_rate,
-    onorm_gain,
-    w_out,
-    norm2_gain,
-    w_gu,
-    w_down,
-    cotangent,
-):
-    f32 = jnp.float32
-    bf16 = jnp.bfloat16
-    local_rows, width = tokens.shape
+F32, BF16 = jnp.float32, jnp.bfloat16
+
+
+def dot(a, b, dims):
+    return lax.dot_general(a, b, (dims, ((), ())), preferred_element_type=F32)
+
+
+def log2(n):
+    return n.bit_length() - 1
+
+
+def low_bit(m, bits):
+    return (m & -m).bit_length() - 1 if m else bits
+
+
+def flip(index, mask):
+    out = index
+    for k in range(mask.bit_length()):
+        if (mask >> k) & 1:
+            out = out + (1 - 2 * ((index // (1 << k)) % 2)) * (1 << k)
+    return out
+
+
+def greet(axes):
+    barrier = pltpu.get_barrier_semaphore()
+    count = 0
+    for axis, size in axes:
+        me = lax.axis_index(axis)
+        for k in range(log2(size)):
+            pl.semaphore_signal(barrier, inc=1, device_id={axis: flip(me, 1 << k)}, device_id_type=MESH)
+            count += 1
+    pl.semaphore_wait(barrier, count)
+
+
+class Gather:
+    def __init__(self, buf, rows, axis, size, send, recv):
+        self.buf, self.rows, self.axis, self.size = buf, rows, axis, size
+        self.send, self.recv = send, recv
+        self.me = lax.axis_index(axis)
+        self.bits = log2(size)
+        self.sent = []
+
+    def block(self, m):
+        return pl.ds(pl.multiple_of(flip(self.me, m) * self.rows, self.rows), self.rows)
+
+    def copy(self, m, k):
+        to = m + (1 << k)
+        at = self.block(m)
+        return pltpu.make_async_remote_copy(
+            src_ref=self.buf.at[at], dst_ref=self.buf.at[at], send_sem=self.send.at[to], recv_sem=self.recv.at[to],
+            device_id={self.axis: flip(self.me, 1 << k)}, device_id_type=MESH,
+        )
+
+    def push(self, m):
+        for k in reversed(range(low_bit(m, self.bits))):
+            copy = self.copy(m, k)
+            copy.start()
+            self.sent.append(copy)
+
+    def arrive(self, m):
+        k = low_bit(m, self.bits)
+        at = self.block(m)
+        pltpu.make_async_remote_copy(
+            src_ref=self.buf.at[at], dst_ref=self.buf.at[at], send_sem=self.send.at[m], recv_sem=self.recv.at[m],
+            device_id={self.axis: flip(self.me, 1 << k)}, device_id_type=MESH,
+        ).wait_recv()
+        self.push(m)
+
+    def close(self):
+        for copy in self.sent:
+            copy.wait_send()
+
+
+class Scatter:
+    def __init__(self, part, out, into, axis, size, send, recv):
+        self.part, self.out, self.into, self.axis, self.size = part, out, into, axis, size
+        self.send, self.recv = send, recv
+        self.me = lax.axis_index(axis)
+        self.bits = log2(size)
+        self.sent = []
+
+    def copy(self, m):
+        return pltpu.make_async_remote_copy(
+            src_ref=self.out.at[m], dst_ref=self.into.at[m], send_sem=self.send.at[m], recv_sem=self.recv.at[m],
+            device_id={self.axis: flip(self.me, 1 << low_bit(m, self.bits))}, device_id_type=MESH,
+        )
+
+    def total(self, m):
+        total = self.part(m)
+        for j in range(low_bit(m, self.bits)):
+            slot = m + (1 << j)
+            self.copy(slot).wait_recv()
+            total = total + self.into[slot].astype(F32)
+        return total
+
+    def begin(self):
+        order = sorted(range(1, self.size), key=lambda m: -int(format(m, f"0{self.bits}b")[::-1], 2))
+        for m in order:
+            self.out[m] = self.total(m).astype(self.out.dtype)
+            copy = self.copy(m)
+            copy.start()
+            self.sent.append(copy)
+
+    def finish(self):
+        return self.total(0)
+
+    def close(self):
+        for copy in self.sent:
+            copy.wait_send()
+
+
+def rms_back(rows, gain, d):
+    scale = lax.rsqrt(jnp.mean(rows * rows, axis=-1, keepdims=True) + 1e-06)
+    dg = d * gain
+    unit = rows * scale
+    d_rows = scale * (dg - unit * jnp.mean(dg * unit, axis=-1, keepdims=True))
+    return d_rows, jnp.sum(d * unit, axis=0, keepdims=True)
+
+
+def entry_kernel(nt, tokens, cot, gain, w_mix, w_gates, rows1, cots, proj, gates, send1, recv1, send2, recv2):
+    rows = tokens.shape[0]
+    one = Gather(rows1, rows, "tensor", nt, send1, recv1)
+    two = Gather(cots, rows, "tensor", nt, send2, recv2)
+    mine = one.block(0)
+    greet([("tensor", nt)])
+    rows1[mine, :] = rms_norm(tokens[...].astype(F32), gain[...]).astype(BF16)
+    one.push(0)
+    cots[mine, :] = cot[...]
+    two.push(0)
+    for m in range(nt):
+        if m:
+            one.arrive(m)
+        at = one.block(m)
+        x = rows1[at, :]
+        proj[at, :] = dot(x, w_mix[...], NN)
+        gates[at, :] = dot(x, w_gates[...], NN)
+    for m in range(1, nt):
+        two.arrive(m)
+    one.close()
+    two.close()
+
+
+def middle_kernel(nt, mixed, cots, tokens, cot, gain, w_out, w_gu, w_down,
+                  out, d_resid, d_gain, d_heads, grads,
+                  rows2, drows, resid, d_act, act, d_gate, d_up, outs, ins, send, recv):
+    rows = tokens.shape[0]
+    hidden = w_down.shape[0]
+    first = Gather(rows2, rows, "tensor", nt, send.at[0], recv.at[0])
+    last = Gather(drows, rows, "tensor", nt, send.at[1], recv.at[1])
+    block = first.block
+    mine = block(0)
+
+    def scatter(part, i):
+        return Scatter(part, outs.at[i], ins.at[i], "tensor", nt, send.at[2 + i], recv.at[2 + i])
+
+    greet([("tensor", nt)])
+    mixing = scatter(lambda m: dot(mixed[block(m), :], w_out[...], NN), 0)
+    mixing.begin()
+    resid[...] = tokens[...].astype(F32) + mixing.finish()
+    rows2[mine, :] = rms_norm(resid[...], gain[...]).astype(BF16)
+    first.push(0)
+
+    def fill(i, carry):
+        at = pl.ds(pl.multiple_of(i * rows, rows), rows)
+        d_act[at, :] = dot(cots[at, :], w_down[...], NT)
+        return carry
+
+    lax.fori_loop(0, nt, fill, 0)
+    for m in range(nt):
+        if m:
+            first.arrive(m)
+        at = block(m)
+        x = rows2[at, :]
+        gate = dot(x, w_gu[0], NT)
+        up = dot(x, w_gu[1], NT)
+        da = d_act[at, :]
+        sig = jax.nn.sigmoid(gate)
+        swish = gate * sig
+        act[at, :] = (swish * up).astype(BF16)
+        d_up[at, :] = (da * swish).astype(BF16)
+        d_gate[at, :] = (da * up * (sig + swish * (1.0 - sig))).astype(BF16)
+    norming = scatter(lambda m: dot(d_gate[block(m), :], w_gu[0], NN) + dot(d_up[block(m), :], w_gu[1], NN), 1)
+    norming.begin()
+    grads[0:hidden, :] = dot(d_gate[...], rows2[...], TN).astype(BF16)
+    grads[hidden : 2 * hidden, :] = dot(d_up[...], rows2[...], TN).astype(BF16)
+    d_res, d_gain[...] = rms_back(resid[...], gain[...], norming.finish())
+    d_res = cot[...].astype(F32) + d_res
+    d_resid[...] = d_res
+    drows[mine, :] = d_res.astype(BF16)
+    last.push(0)
+    closing = scatter(lambda m: dot(act[block(m), :], w_down[...], NN), 2)
+    closing.begin()
+    grads[2 * hidden : 3 * hidden, :] = dot(act[...], cots[...], TN).astype(BF16)
+    for m in range(nt):
+        if m:
+            last.arrive(m)
+        at = block(m)
+        d_heads[at, :] = dot(drows[at, :], w_out[...], NT)
+    grads[3 * hidden :, :] = dot(mixed[...], drows[...], TN).astype(BF16)
+    out[...] = (resid[...] + closing.finish()).astype(BF16)
+    for group in (mixing, first, norming, last, closing):
+        group.close()
+
+
+class Share:
+    def __init__(self, source, sink, out, into, fwd, nd, order, send, recv):
+        self.source, self.sink, self.out, self.into, self.fwd = source, sink, out, into, fwd
+        self.order, self.send, self.recv = order, send, recv
+        self.bits = len(order)
+        self.size = nd
+        self.me = lax.axis_index("dp")
+        self.sent = []
+
+    def real(self, m):
+        return sum(1 << self.order[k] for k in range(self.bits) if (m >> k) & 1)
+
+    def ref(self, m):
+        return self.source(flip(self.me, self.real(m)))
+
+    def stage(self, s):
+        names = [m for m in range(1, self.size) if low_bit(m, self.bits) == s]
+        return sorted(names, key=lambda m: -int(format(m, f"0{self.bits}b")[::-1], 2))
+
+    def copy(self, m):
+        s = low_bit(m, self.bits)
+        src = self.fwd.at[(m >> 1) - 1] if s else self.ref(m)
+        return pltpu.make_async_remote_copy(
+            src_ref=src, dst_ref=self.into.at[m - 1], send_sem=self.send.at[m], recv_sem=self.recv.at[m],
+            device_id={"dp": flip(self.me, 1 << self.order[s])}, device_id_type=MESH,
+        )
+
+    def total(self, m):
+        total = self.ref(m)[...].astype(F32)
+        for j in range(low_bit(m, self.bits)):
+            slot = m + (1 << j)
+            self.copy(slot).wait_recv()
+            total = total + self.into[slot - 1].astype(F32)
+        return total
+
+    def run(self, s):
+        if s == self.bits:
+            self.sink(self.total(0))
+            return
+        for m in self.stage(s):
+            if s:
+                self.fwd[(m >> 1) - 1] = self.total(m).astype(BF16)
+            copy = self.copy(m)
+            copy.start()
+            self.sent.append(copy)
+
+    def close(self):
+        for copy in self.sent:
+            copy.wait_send()
+
+
+def orders(bits):
+    plain = tuple(range(bits))
+    return plain, (1, 0) + plain[2:] if bits > 1 else plain
+
+
+def exit_kernel(nt, nd, cuts, rows1, d_proj, d_gates, w_mix, w_gates, tokens, gain, d_resid, grads,
+                d_conv, d_rate, d_onorm, d_gain2,
+                d_tokens, g_mix, g_gates, g_cols, g_small,
+                gm, gg, outs, ins, send, recv, small, small_in, small_send, small_recv,
+                mix_in, mix_fwd, gate_in, gate_fwd, col_in, col_fwd, dp_send, dp_recv):
+    rows, width = tokens.shape
+    share = width // nd
+    bits, tbits = log2(nd), log2(nt)
+    plain, swapped = orders(bits)
+    greet([("tensor", nt), ("dp", nd)])
+    shares = []
+
+    def column(i, start, stop):
+        def source(b):
+            return grads.at[start:stop, pl.ds(pl.multiple_of(b * share, share), share)]
+
+        def sink(total):
+            g_cols[start:stop, :] = total
+
+        def part(ref):
+            return ref.at[:, start:stop, :]
+
+        return Share(source, sink, None, part(col_in), part(col_fwd), nd,
+                     swapped if i == 0 else plain, dp_send.at[i], dp_recv.at[i])
+
+    for i, (start, stop) in enumerate(cuts):
+        shares.append(column(i, start, stop))
+    count = len(shares)
+
+    def mix_sink(total):
+        g_mix[...] = total
+
+    def gates_sink(total):
+        g_gates[...] = total
+
+    mix_share = Share(lambda b: gm.at[b], mix_sink, None, mix_in, mix_fwd, nd, plain, dp_send.at[count], dp_recv.at[count])
+    gates_share = Share(lambda b: gg.at[b], gates_sink, None, gate_in, gate_fwd, nd, plain, dp_send.at[count + 1], dp_recv.at[count + 1])
+    for one in shares:
+        one.run(0)
+
+    def block(m):
+        return pl.ds(pl.multiple_of(flip(lax.axis_index("tensor"), m) * rows, rows), rows)
+
+    norming = Scatter(
+        lambda m: dot(d_proj[block(m), :], w_mix[...], NT) + dot(d_gates[block(m), :], w_gates[...], NT),
+        outs, ins, "tensor", nt, send, recv,
+    )
+    norming.begin()
+
+    def fill(b, carry):
+        lhs = rows1[:, pl.ds(pl.multiple_of(b * share, share), share)]
+        gm[b] = dot(lhs, d_proj[...], TN).astype(BF16)
+        gg[b] = dot(lhs, d_gates[...], TN).astype(BF16)
+        return carry
+
+    lax.fori_loop(0, nd, fill, 0)
+    shares = shares[:-1] + [mix_share, shares[-1], gates_share]
+    mix_share.run(0)
+    gates_share.run(0)
+
+    d_res, gain_part = rms_back(tokens[...].astype(F32), gain[...], norming.finish())
+    d_tokens[...] = (d_resid[...] + d_res).astype(BF16)
+
+    small[0] = jnp.zeros(small.shape[1:], F32)
+    conv_rows, conv_width = d_conv.shape
+    small[0, 0:1, 0:width] = gain_part
+    small[0, 1:2, 0:width] = d_gain2[...]
+    heads, value = d_onorm.shape
+    for h in range(heads):
+        small[0, 2:3, h * value : (h + 1) * value] = d_onorm[h : h + 1, :]
+        small[0, 3:4, h * LANES : (h + 1) * LANES] = d_rate[h : h + 1, :]
+    small[0, 4 : 4 + conv_rows, 0:conv_width] = d_conv[...]
+
+    hops = [("tensor", k) for k in range(tbits)] + [("dp", k) for k in reversed(range(bits))]
+
+    def small_copy(i):
+        axis, k = hops[i]
+        return pltpu.make_async_remote_copy(
+            src_ref=small.at[i], dst_ref=small_in.at[i], send_sem=small_send.at[i], recv_sem=small_recv.at[i],
+            device_id={axis: flip(lax.axis_index(axis), 1 << k)}, device_id_type=MESH,
+        )
+
+    def small_start(i):
+        small_copy(i).start()
+
+    def small_finish(i):
+        small_copy(i).wait_recv()
+        got = small_in[i]
+        if hops[i][0] == "tensor":
+            place = lax.broadcasted_iota(jnp.int32, got.shape, 0)
+            got = jnp.where(place < 2, got, 0.0)
+        small[i + 1] = small[i] + got
+
+    small_start(0)
+    for i in range(tbits):
+        small_finish(i)
+        small_start(i + 1)
+    pending = tbits
+    for step in range(len(shares) + bits - 1):
+        for s in reversed(range(1, bits)):
+            a = step - (s - 1)
+            if 0 <= a < len(shares):
+                shares[a].run(s)
+        a = step - (bits - 1)
+        if 0 <= a < len(shares):
+            shares[a].run(bits)
+        if step >= 1 and pending < len(hops):
+            small_finish(pending)
+            pending += 1
+            if pending < len(hops):
+                small_start(pending)
+    while pending < len(hops):
+        small_finish(pending)
+        pending += 1
+        if pending < len(hops):
+            small_start(pending)
+    g_small[...] = small[len(hops)]
+    for i in range(len(hops)):
+        small_copy(i).wait_send()
+    norming.close()
+    for one in shares:
+        one.close()
+
+
+def exit_plain_kernel(nt, rows1, d_proj, d_gates, w_mix, w_gates, tokens, gain, d_resid,
+                      d_tokens, gain_part, gm, gg, outs, ins, send, recv):
+    rows = tokens.shape[0]
+    greet([("tensor", nt)])
+
+    def block(m):
+        return pl.ds(pl.multiple_of(flip(lax.axis_index("tensor"), m) * rows, rows), rows)
+
+    norming = Scatter(
+        lambda m: dot(d_proj[block(m), :], w_mix[...], NT) + dot(d_gates[block(m), :], w_gates[...], NT),
+        outs, ins, "tensor", nt, send, recv,
+    )
+    norming.begin()
+
+    def fill(b, carry):
+        at = pl.ds(pl.multiple_of(b * LANES, LANES), LANES)
+        lhs = rows1[:, at]
+        gm[at, :] = dot(lhs, d_proj[...], TN).astype(BF16)
+        gg[at, :] = dot(lhs, d_gates[...], TN).astype(BF16)
+        return carry
+
+    lax.fori_loop(0, rows1.shape[1] // LANES, fill, 0)
+    d_res, gain_part[...] = rms_back(tokens[...].astype(F32), gain[...], norming.finish())
+    d_tokens[...] = (d_resid[...] + d_res).astype(BF16)
+    norming.close()
+
+
+def call(kernel, outs, scratch, name, collective_id, args):
+    return pl.pallas_call(
+        kernel,
+        out_shape=[jax.ShapeDtypeStruct(s, d) for s, d in outs],
+        in_specs=[VMEM] * len(args),
+        out_specs=[VMEM] * len(outs),
+        scratch_shapes=scratch,
+        compiler_params=pltpu.CompilerParams(
+            collective_id=collective_id, has_side_effects=True, vmem_limit_bytes=60 * 1024 * 1024
+        ),
+        name=name,
+    )(*args)
+
+
+def local(nt, nd, tokens, seg_starts, norm1_gain, w_mix, w_gates, conv_w, decay_rate, onorm_gain, w_out, norm2_gain,
+          w_gu, w_down, cotangent):
+    rows, width = tokens.shape
     seqs = seg_starts.shape[0]
-    heads = w_mix.shape[1]
-    mix_cols = w_mix.shape[2]
-    value_width = onorm_gain.shape[1]
+    heads, mix_cols = w_mix.shape[1], w_mix.shape[2]
+    value = onorm_gain.shape[1]
     hidden = w_down.shape[0]
+    conv = conv_w.shape[2]
+    total = rows * nt
+    length = total // seqs
+    dma = pltpu.SemaphoreType.DMA
     mix2d = w_mix.reshape(width, heads * mix_cols)
-    gates2d = w_gates.reshape(width, heads * 2)
-    out2d = w_out.reshape(heads * value_width, width)
-    gu2d = w_gu.reshape(width, 2 * hidden)
-    resid = tokens.astype(f32)
-    normed1 = rms_norm(resid, norm1_gain).astype(bf16)
-    rows1 = lax.all_gather(normed1, "tensor", axis=0, tiled=True)
-    total_rows = rows1.shape[0]
-    length = total_rows // seqs
-    dims = (heads, mix_cols, conv_w.shape[2], value_width)
-    proj = jnp.dot(rows1, mix2d, preferred_element_type=f32)
-    gates_pre = jnp.dot(rows1, gates2d, preferred_element_type=f32)
-    aux = jax.vmap(segment_ids, in_axes=(0, None))(seg_starts, length).reshape(total_rows, 8)
+    gates2d = jnp.pad(w_gates.reshape(width, heads * 2), ((0, 0), (0, LANES - 2 * heads)))
+    out2d = w_out.reshape(heads * value, width)
+    gu = jnp.transpose(w_gu, (1, 2, 0))
+    gain1, gain2 = norm1_gain[None, :], norm2_gain[None, :]
+    rows1, cots, proj, gates_pre = call(
+        functools.partial(entry_kernel, nt),
+        [((total, width), BF16), ((total, width), BF16), ((total, heads * mix_cols), F32), ((total, LANES), F32)],
+        [dma((nt,))] * 4,
+        "entry", 0, (tokens, cotangent, gain1, mix2d, gates2d),
+    )
+    aux = jax.vmap(segment_ids, in_axes=(0, None))(seg_starts, length).reshape(total, 8)
+    dims = (heads, mix_cols, conv, value)
     mixer_args = (proj, gates_pre, aux, conv_w.reshape(4, -1), decay_rate[None, :], onorm_gain)
     mixed, states, inverses = mixer_forward(*mixer_args, dims, seqs)
-    cot_rows = lax.all_gather(cotangent, "tensor", axis=0, tiled=True)
-    mixed, cot_rows = lax.optimization_barrier((mixed, cot_rows))
-    resid2 = resid + lax.psum_scatter(
-        jnp.dot(mixed, out2d, preferred_element_type=f32).astype(jnp.bfloat16),
-        "tensor",
-        scatter_dimension=0,
-        tiled=True,
-    ).astype(jnp.float32)
-    normed2 = rms_norm(resid2, norm2_gain).astype(bf16)
-    rows2 = lax.all_gather(normed2, "tensor", axis=0, tiled=True)
-    gu = jnp.dot(rows2, gu2d, preferred_element_type=f32).reshape(total_rows, 2, hidden)
-    act = swish_gate(gu[:, 0], gu[:, 1]).astype(bf16)
-    ffn_part = jnp.dot(act, w_down, preferred_element_type=f32).astype(bf16)
-    grad_down = jnp.dot(cot_rows.T, act, preferred_element_type=f32).astype(bf16)
-    d_act = jnp.dot(cot_rows, w_down.T, preferred_element_type=f32)
-    _, swish_back = jax.vjp(swish_gate, gu[:, 0], gu[:, 1])
-    d_gate, d_up = swish_back(d_act)
-    d_gu = jnp.stack([d_gate, d_up], axis=1).astype(bf16).reshape(total_rows, 2 * hidden)
-    grad_gu = jnp.dot(rows2.T, d_gu, preferred_element_type=f32).astype(bf16)
-    d_normed2 = lax.psum_scatter(
-        jnp.dot(d_gu, gu2d.T, preferred_element_type=f32).astype(jnp.bfloat16),
-        "tensor",
-        scatter_dimension=0,
-        tiled=True,
-    ).astype(jnp.float32)
-    _, norm2_back = jax.vjp(rms_norm, resid2, norm2_gain)
-    d_resid_ffn, gain2_part = norm2_back(d_normed2)
-    d_resid2 = cotangent.astype(f32) + d_resid_ffn
-    d_rows = lax.all_gather(d_resid2.astype(bf16), "tensor", axis=0, tiled=True)
-    grad_out = jnp.dot(d_rows.T, mixed, preferred_element_type=f32).astype(bf16)
-    d_heads = jnp.dot(d_rows, out2d.T, preferred_element_type=f32)
-    d_heads, ffn_part = lax.optimization_barrier((d_heads, ffn_part))
-    ffn_sum = lax.psum_scatter(ffn_part, "tensor", scatter_dimension=0, tiled=True)
-    d_proj_b, d_gates_b, d_conv, d_rate, d_onorm = mixer_backward(
-        *mixer_args, states, inverses, d_heads, dims, seqs
+    block = pltpu.VMEM((total, hidden), BF16)
+    output, d_resid2, d_gain2, d_heads, grads = call(
+        functools.partial(middle_kernel, nt),
+        [((rows, width), BF16), ((rows, width), F32), ((1, width), F32), ((total, heads * value), F32),
+         ((3 * hidden + heads * value, width), BF16)],
+        [pltpu.VMEM((total, width), BF16), pltpu.VMEM((total, width), BF16), pltpu.VMEM((rows, width), F32),
+         pltpu.VMEM((total, hidden), F32), block, block, block,
+         pltpu.VMEM((3, nt, rows, width), BF16), pltpu.VMEM((3, nt, rows, width), BF16), dma((5, nt)), dma((5, nt))],
+        "middle", 1, (mixed, cots, tokens, cotangent, gain2, out2d, gu, w_down),
     )
-    d_proj_b, ffn_sum = lax.optimization_barrier((d_proj_b, ffn_sum))
-    output = (resid2 + ffn_sum.astype(f32)).astype(bf16)
-    d_conv = d_conv.reshape(conv_w.shape)
-    d_rate = d_rate[:, 0]
-    grad_mix = jnp.dot(rows1.T, d_proj_b, preferred_element_type=f32).astype(bf16)
-    grad_gates = jnp.dot(rows1.T, d_gates_b, preferred_element_type=f32).astype(bf16)
-    d_normed1 = lax.psum_scatter(
-        (
-            jnp.dot(d_proj_b, mix2d.T, preferred_element_type=f32)
-            + jnp.dot(d_gates_b, gates2d.T, preferred_element_type=f32)
-        ).astype(jnp.bfloat16),
-        "tensor",
-        scatter_dimension=0,
-        tiled=True,
-    ).astype(jnp.float32)
-    pad = -(2 * heads) % 128
-    grads = jnp.concatenate(
-        [grad_mix, grad_gu, grad_down, grad_out, jnp.pad(grad_gates, ((0, 0), (0, pad)))], axis=1
-    )
-    d_normed1, grads = lax.optimization_barrier((d_normed1, grads))
-    _, norm1_back = jax.vjp(rms_norm, resid, norm1_gain)
-    d_resid1, gain1_part = norm1_back(d_normed1)
-    grad_tokens = (d_resid2 + d_resid1).astype(bf16)
-    grad_conv, grad_rate, grad_onorm = lax.psum((d_conv, d_rate, d_onorm), "dp")
-    shares = lax.psum_scatter(grads, "dp", scatter_dimension=0, tiled=True).astype(f32)
-    cuts = []
-    place = 0
-    for size in (heads * mix_cols, 2 * hidden, hidden, heads * value_width, 2 * heads):
-        cuts.append(shares[:, place : place + size])
-        place += size
-    mix_share = cuts[0].reshape(-1, heads, mix_cols)
-    gu_share = cuts[1].reshape(-1, 2, hidden)
-    down_share = cuts[2].T
-    out_share = cuts[3].T.reshape(heads, value_width, -1)
-    gates_share = cuts[4].reshape(-1, heads, 2)
-    gain1_share = lax.psum_scatter(gain1_part, "dp", scatter_dimension=0, tiled=True)
-    gain2_share = lax.psum_scatter(gain2_part, "dp", scatter_dimension=0, tiled=True)
-    gain1_total, gain2_total = lax.psum((gain1_share, gain2_share), "tensor")
+    d_proj, d_gates, d_conv, d_rate, d_onorm = mixer_backward(*mixer_args, states, inverses, d_heads, dims, seqs)
+    share = width // nd
+    exit_args = (rows1, d_proj, d_gates, mix2d, gates2d, tokens, gain1, d_resid2)
+    half = pltpu.VMEM((nt, rows, width), BF16)
+    ends = [0, hidden, 2 * hidden, 3 * hidden, 3 * hidden + heads * value]
+    if share % LANES == 0 and nd > 1 and nd & (nd - 1) == 0:
+        cuts = tuple(zip(ends[:-1], ends[1:]))
+        cols = ends[-1]
+        place = max(width, heads * conv)
+        hops = log2(nt) + log2(nd)
+        mix = heads * mix_cols
+        grad_tokens, g_mix, g_gates, g_cols, g_small = call(
+            functools.partial(exit_kernel, nt, nd, cuts),
+            [((rows, width), BF16), ((share, mix), F32), ((share, LANES), F32), ((cols, share), F32), ((8, place), F32)],
+            [pltpu.VMEM((nd, share, mix), BF16), pltpu.VMEM((nd, share, LANES), BF16), half, half, dma((nt,)), dma((nt,)),
+             pltpu.VMEM((hops + 1, 8, place), F32), pltpu.VMEM((hops, 8, place), F32), dma((hops,)), dma((hops,)),
+             pltpu.VMEM((nd - 1, share, mix), BF16), pltpu.VMEM((nd // 2 - 1, share, mix), BF16),
+             pltpu.VMEM((nd - 1, share, LANES), BF16), pltpu.VMEM((nd // 2 - 1, share, LANES), BF16),
+             pltpu.VMEM((nd - 1, cols, share), BF16), pltpu.VMEM((nd // 2 - 1, cols, share), BF16),
+             dma((len(cuts) + 2, nd)), dma((len(cuts) + 2, nd))],
+            "exit", 2, exit_args + (grads, d_conv, d_rate, d_onorm, d_gain2),
+        )
+        at = lax.axis_index("dp") * share
+        gain1_total = lax.dynamic_slice(g_small[0, :width], (at,), (share,))
+        gain2_total = lax.dynamic_slice(g_small[1, :width], (at,), (share,))
+        grad_onorm = g_small[2, : heads * value].reshape(heads, value)
+        grad_rate = g_small[3, : heads * LANES].reshape(heads, LANES)[:, 0]
+        grad_conv = g_small[4:8, : heads * conv].reshape(conv_w.shape)
+    else:
+        grad_tokens, gain1_part, gm, gg = call(
+            functools.partial(exit_plain_kernel, nt),
+            [((rows, width), BF16), ((1, width), F32), ((width, heads * mix_cols), BF16), ((width, LANES), BF16)],
+            [half, half, dma((nt,)), dma((nt,))],
+            "exit", 2, exit_args,
+        )
+        scatter = functools.partial(lax.psum_scatter, axis_name="dp", tiled=True)
+        g_mix = scatter(gm, scatter_dimension=0).astype(F32)
+        g_gates = scatter(gg, scatter_dimension=0).astype(F32)
+        g_cols = scatter(grads, scatter_dimension=1).astype(F32)
+        gain1_total, gain2_total = lax.psum(
+            (scatter(gain1_part[0], scatter_dimension=0), scatter(d_gain2[0], scatter_dimension=0)), "tensor"
+        )
+        grad_conv, grad_rate, grad_onorm = lax.psum((d_conv.reshape(conv_w.shape), d_rate[:, 0], d_onorm), "dp")
     return (
         output,
         grad_tokens,
         gain1_total,
-        mix_share,
-        gates_share,
+        g_mix.reshape(-1, heads, mix_cols),
+        g_gates[:, : 2 * heads].reshape(-1, heads, 2),
         grad_conv,
         grad_rate,
         grad_onorm,
-        out_share,
+        g_cols[ends[3] : ends[4]].reshape(heads, value, -1),
         gain2_total,
-        gu_share,
-        down_share,
+        jnp.transpose(g_cols[: ends[2]].reshape(2, hidden, -1), (2, 0, 1)),
+        g_cols[ends[2] : ends[3]],
     )
 
 
@@ -593,4 +984,5 @@
         P("dp", None, "tensor"),
         P("tensor", "dp"),
     )
-    return jax.shard_map(local, mesh=mesh, in_specs=in_specs, out_specs=out_specs, check_vma=False)
+    body = functools.partial(local, mesh.shape["tensor"], mesh.shape["dp"])
+    return jax.shard_map(body, mesh=mesh, in_specs=in_specs, out_specs=out_specs, check_vma=False)

time: 407 us -> 311 us (0.76)
  Pallas kernels: 51.8 us -> 285 us
  waiting for transfers between devices: 195 us -> 0 us
  blocking collectives: 46.6 us -> 0 us
  matrix products: 42.8 us -> 0 us
  other arithmetic: 16.8 us -> 1.4 us
  between operations: 15 us -> 0.76 us
  local copies, waits for them, and re-layouts: 37.7 us -> 23.9 us
    pallas_call x0 -> x3, Pallas kernels: none -> 233 us  [call(): pl.pallas_call(kernel, out_shape=[jax.ShapeDtypeStruct(s, d) for s, d in...]
    reduce_scatter x5 -> x0, waiting for transfers between devices: 155 us -> none  [the longest x1 106 us: local(): lax.psum_scatter(grads, 'dp', scatter_dimension=0, tiled=True).astype(f32)]
    dot_general x15 -> x0, matrix products: 42.8 us -> none  [the longest x1 5.7 us: local(): proj = jnp.dot(rows1, mix2d, preferred_element_type=f32)]
    unnamed x1 -> x0, blocking collectives: 40 us -> none
    all_gather x4 -> x0, waiting for transfers between devices: 38.6 us -> none  [the longest x1 16.8 us: local(): rows2 = lax.all_gather(normed2, 'tensor', axis=0, tiled=True)]
    concatenate x1 -> x0, local copies, waits for them, and re-layouts: 13.7 us -> none  [local(): jnp.concatenate([grad_mix, grad_gu, grad_down, grad_out, jnp.pad(grad_gat...]
    convert_element_type x8 -> x0, other arithmetic: 10.9 us -> none  [the longest x1 1.95 us: local(): d_rows = lax.all_gather(d_resid2.astype(bf16), 'tensor', axis=0, tiled=True)]
    psum x1 -> x0, blocking collectives: 6.54 us -> none  [local(): gain1_total, gain2_total = lax.psum((gain1_share, gain2_share), 'tensor')]
  transfers between devices with their start and end apart: 9 -> 0, of which waited for: 6 -> 0; matrix products, arithmetic and copies ran while one was open for 14% -> 0% of each run, Pallas kernels for 13% -> 0%
where the time goes in v1:
time: 311 us
  Pallas kernels  285 us (92%)
  local copies, waits for them, and re-layouts  23.9 us (8%)
    pallas_call x3, Pallas kernels, call(): pl.pallas_call(kernel, out_shape=[jax.ShapeDtypeStruct(s, d) for s, d in...  233 us
    pallas_call x1, Pallas kernels, mixer_backward(): pl.pallas_call(functools.partial(backward_kernel, dims), grid=(seqs, bloc...  27.1 us
    pallas_call x1, Pallas kernels, mixer_forward(): pl.pallas_call(functools.partial(forward_kernel, dims), grid=(seqs, block...  24.9 us
    unnamed x15, local copies, waits for them, and re-layouts  6.79 us

profile of v1, /device:TPU:0, one launch (start us, length us, event | category | flops | bytes accessed | tf_op | source)
XLA Modules:
  0.0 310.8 jit_solution(18109785677419605982)
XLA Ops:
  0.6 0.0 copy-start.3
  0.7 4.2 %copy.46 = bf16[128,8,2,768]{3,1,2,0:T(8,128)(2,1)} copy(bf16[128,8,2,768]{3,2,1,0:T(2,128)(2,1)} %bitcast.45) | data formatting | bytes 6291456
  4.8 0.0 copy-start.4
  4.8 0.0 copy-start.2
  4.8 0.0 copy-done.3
  4.8 0.2 copy.41
  5.0 0.8 pad.16.w_gates
  5.8 21.6 %entry.1 = (bf16[512,1024]{1,0:T(8,128)(2,1)}, bf16[512,1024]{1,0:T(8,128)(2,1)}, f32[512,1536]{1,0:T(8,128)}, f32[512,128]{1,0:T(8,128)}) custom-call(bf16[128,1024]{1,0:T(8,128)(2,1)} %tokens.5, bf16[128,1024]{1,0:T(8,128)(2,1)} %cot.3, f32[1,1024]{1,0:T(1,128)} %bitcast.60, bf16[1024,1536]{1,0:T(8,128)(2,1)} %bitcast.43, bf16[1024,128]{1,0:T(8,128)(2,1)} %pad.16.w_gates), custom_call_target="tpu_custom_call" | custom-call | tf_op jit(solution)/shard_map/entry/pallas_call | solution.py:849
  27.4 0.0 copy-done.4
  27.4 0.1 fusion
  27.5 0.3 reduce-window.6
  27.8 0.2 slice_reduce_fusion.1
  28.0 0.2 reduce-window.9
  28.2 0.1 broadcast.51
  28.3 0.1 fusion.3
  28.4 0.5 slice.75
  28.9 0.7 pad_add_fusion
  29.6 0.1 slice.63
  29.7 0.1 broadcast_in_dim.20
  29.8 0.1 broadcast_in_dim.21
  29.9 0.8 copy.42
  30.7 0.0 copy-done.2
  30.7 0.6 copy.47
  31.4 24.9 %mixer_forward.1 = (bf16[512,512]{1,0:T(8,128)(2,1)}, f32[8,256,256]{2,1,0:T(8,128)}, f32[8,128,64]{2,1,0:T(8,128)}) custom-call(f32[512,1536]{1,0:T(8,128)} %get-tuple-element.34.halo_ref.proj_ref, f32[512,1536]{1,0:T(8,128)} %get-tuple-element.34.halo_ref.proj_ref, f32[512,128]{1,0:T(8,128)} %get-tuple-element.35.gates_ref, f32[512,8]{1,0:T(8,128)} %bitcast.50, ...), custom_call_target="tpu_custom_call" | custom-call | flops 2048000000 | bytes 8388608 | tf_op jit(solution)/shard_map/mixer_forward/pallas_call | solution.py:378
  56.2 49.5 %middle.1 = (bf16[128,1024]{1,0:T(8,128)(2,1)}, f32[128,1024]{1,0:T(8,128)}, f32[1,1024]{1,0:T(1,128)}, f32[512,512]{1,0:T(8,128)}, bf16[2624,1024]{1,0:T(8,128)(2,1)}) custom-call(bf16[512,512]{1,0:T(8,128)(2,1)} %get-tuple-element.36.mixed, bf16[512,1024]{1,0:T(8,128)(2,1)} %get-tuple-element.37.cots, bf16[128,1024]{1,0:T(8,128)(2,1)} %tokens.5, ...), custom_call_target="tpu_custom_call" | custom-call | tf_op jit(solution)/shard_map/middle/pallas_call | solution.py:849
  105.8 27.1 %mixer_backward.1 = (bf16[512,1536]{1,0:T(8,128)(2,1)}, bf16[512,128]{1,0:T(8,128)(2,1)}, f32[4,1024]{1,0:T(4,128)}, f32[2,128]{1,0:T(2,128)}, f32[2,256]{1,0:T(2,128)}) custom-call(f32[512,1536]{1,0:T(8,128)} %get-tuple-element.34.halo_ref.proj_ref, f32[512,1536]{1,0:T(8,128)} %get-tuple-element.34.halo_ref.proj_ref, ...), custom_call_target="tpu_custom_call" | custom-call | flops 5120000000 | bytes 12582912 | tf_op jit(solution)/shard_map/mixer_backward/pallas_call | solution.py:405
  132.9 161.6 %exit.1 = (bf16[128,1024]{1,0:T(8,128)(2,1)}, f32[128,1536]{1,0:T(8,128)}, f32[128,128]{1,0:T(8,128)}, f32[2624,128]{1,0:T(8,128)}, f32[8,1024]{1,0:T(8,128)}) custom-call(bf16[512,1024]{1,0:T(8,128)(2,1)} %get-tuple-element.39.rows1, bf16[512,1536]{1,0:T(8,128)(2,1)} %get-tuple-element.43.d_proj, bf16[512,128]{1,0:T(8,128)(2,1)} %get-tuple-element.44.d_gates, ...), custom_call_target="tpu_custom_call" | custom-call | tf_op jit(solution)/shard_map/exit/pallas_call | solution.py:849
  294.5 0.0 copy-start
  294.6 0.0 copy-start.1
  294.6 0.8 fusion.4
  295.4 0.5 dynamic-slice_bitcast_fusion
  295.9 2.5 reshape.231
  298.5 1.5 copy.43
  299.9 0.8 slice.67
  300.7 0.6 reshape.233
  301.3 0.7 slice.68
  302.0 0.6 copy.45
  302.6 0.7 slice_reduce_fusion
  303.4 0.6 reshape_squeeze.7
  304.0 1.7 slice.71
  305.6 2.0 slice.73
  307.6 1.7 slice.74
  309.4 0.0 copy-done
  309.4 0.7 copy.50
  310.1 0.0 copy-done.1
  310.1 0.7 copy.51
  (9 shorter events, 0.1 us)
Async XLA Ops:
  0.6 4.2 %copy-start.3 = (bf16[1024,2,2]{0,2,1:T(2,128)(2,1)S(1)}, bf16[1024,2,2]{0,2,1:T(2,128)(2,1)}, u32[]{:S(2)}) copy-start(bf16[1024,2,2]{0,2,1:T(2,128)(2,1)} %param.17) | copy-start | bytes 24580
  4.8 22.6 %copy-start.4 = (s32[1,6]{1,0:T(1,128)S(1)}, s32[1,6]{1,0:T(1,128)}, u32[]{:S(2)}) copy-start(s32[1,6]{1,0:T(1,128)} %param.14) | copy-start | bytes 76
  4.8 25.9 %copy-start.2 = (f32[4,2,512]{2,1,0:T(2,128)S(1)}, f32[4,2,512]{2,1,0:T(2,128)}, u32[]{:S(2)}) copy-start(f32[4,2,512]{2,1,0:T(2,128)} %param.18) | copy-start | bytes 49156
  294.5 14.8 %copy-start = (bf16[128,1024]{1,0:T(8,128)(2,1)S(1)}, bf16[128,1024]{1,0:T(8,128)(2,1)}, u32[]{:S(2)}) copy-start(bf16[128,1024]{1,0:T(8,128)(2,1)} %get-tuple-element.87) | copy-start | bytes 786436
  294.6 15.5 %copy-start.1 = (bf16[128,1024]{1,0:T(8,128)(2,1)S(1)}, bf16[128,1024]{1,0:T(8,128)(2,1)}, u32[]{:S(2)}) copy-start(bf16[128,1024]{1,0:T(8,128)(2,1)} %get-tuple-element.88) | copy-start | bytes 786436

commit v2 on v1

--- a/solution.py
+++ b/solution.py
@@ -576,9 +576,14 @@
     two.close()
 
 
-def middle_kernel(nt, mixed, cots, tokens, cot, gain, w_out, w_gu, w_down,
-                  out, d_resid, d_gain, d_heads, grads,
-                  rows2, drows, resid, d_act, act, d_gate, d_up, outs, ins, send, recv):
+def columns_of(ref, start, stop, share):
+    return lambda b: ref.at[start:stop, pl.ds(pl.multiple_of(b * share, share), share)]
+
+
+def middle_kernel(nt, nd, ring, mixed, cots, tokens, cot, gain, w_out, w_gu, w_down,
+                  out, d_resid, d_gain, d_heads, grads, *rest):
+    got = rest[:2] if ring else ()
+    rows2, drows, resid, d_act, act, d_gate, d_up, outs, ins, send, recv, dp_send, dp_recv = rest[len(got) :]
     rows = tokens.shape[0]
     hidden = w_down.shape[0]
     first = Gather(rows2, rows, "tensor", nt, send.at[0], recv.at[0])
@@ -589,7 +594,7 @@
     def scatter(part, i):
         return Scatter(part, outs.at[i], ins.at[i], "tensor", nt, send.at[2 + i], recv.at[2 + i])
 
-    greet([("tensor", nt)])
+    greet([("tensor", nt), ("dp", nd)] if ring else [("tensor", nt)])
     mixing = scatter(lambda m: dot(mixed[block(m), :], w_out[...], NN), 0)
     mixing.begin()
     resid[...] = tokens[...].astype(F32) + mixing.finish()
@@ -619,6 +624,13 @@
     norming.begin()
     grads[0:hidden, :] = dot(d_gate[...], rows2[...], TN).astype(BF16)
     grads[hidden : 2 * hidden, :] = dot(d_up[...], rows2[...], TN).astype(BF16)
+    shares = []
+    if ring:
+        share = rows2.shape[1] // nd
+        for i, order in enumerate(reversed(orders(log2(nd)))):
+            source = columns_of(grads, i * hidden, (i + 1) * hidden, share)
+            shares.append(Share(source, None, got[i], None, None, nd, order, dp_send.at[i], dp_recv.at[i]))
+            shares[i].run(0)
     d_res, d_gain[...] = rms_back(resid[...], gain[...], norming.finish())
     d_res = cot[...].astype(F32) + d_res
     d_resid[...] = d_res
@@ -634,14 +646,16 @@
         d_heads[at, :] = dot(drows[at, :], w_out[...], NT)
     grads[3 * hidden :, :] = dot(mixed[...], drows[...], TN).astype(BF16)
     out[...] = (resid[...] + closing.finish()).astype(BF16)
-    for group in (mixing, first, norming, last, closing):
+    for one in shares:
+        one.receive(0)
+    for group in (mixing, first, norming, last, closing, *shares):
         group.close()
 
 
 class Share:
-    def __init__(self, source, sink, out, into, fwd, nd, order, send, recv):
-        self.source, self.sink, self.out, self.into, self.fwd = source, sink, out, into, fwd
-        self.order, self.send, self.recv = order, send, recv
+    def __init__(self, source, sink, first, into, fwd, nd, order, send, recv, got=False):
+        self.source, self.sink, self.first, self.into, self.fwd = source, sink, first, into, fwd
+        self.order, self.send, self.recv, self.got = order, send, recv, got
         self.bits = len(order)
         self.size = nd
         self.me = lax.axis_index("dp")
@@ -657,11 +671,14 @@
         names = [m for m in range(1, self.size) if low_bit(m, self.bits) == s]
         return sorted(names, key=lambda m: -int(format(m, f"0{self.bits}b")[::-1], 2))
 
+    def slot(self, m):
+        return self.first.at[m >> 1] if m & 1 else self.into.at[(m >> 1) - 1]
+
     def copy(self, m):
         s = low_bit(m, self.bits)
-        src = self.fwd.at[(m >> 1) - 1] if s else self.ref(m)
         return pltpu.make_async_remote_copy(
-            src_ref=src, dst_ref=self.into.at[m - 1], send_sem=self.send.at[m], recv_sem=self.recv.at[m],
+            src_ref=self.fwd.at[(m >> 1) - 1] if s else self.ref(m), dst_ref=self.slot(m),
+            send_sem=self.send.at[m], recv_sem=self.recv.at[m],
             device_id={"dp": flip(self.me, 1 << self.order[s])}, device_id_type=MESH,
         )
 
@@ -669,8 +686,9 @@
         total = self.ref(m)[...].astype(F32)
         for j in range(low_bit(m, self.bits)):
             slot = m + (1 << j)
-            self.copy(slot).wait_recv()
-            total = total + self.into[slot - 1].astype(F32)
+            if j or not self.got:
+                self.copy(slot).wait_recv()
+            total = total + self.slot(slot)[...].astype(F32)
         return total
 
     def run(self, s):
@@ -684,6 +702,10 @@
             copy.start()
             self.sent.append(copy)
 
+    def receive(self, s):
+        for m in self.stage(s):
+            self.copy(m).wait_recv()
+
     def close(self):
         for copy in self.sent:
             copy.wait_send()
@@ -695,44 +717,41 @@
 
 
 def exit_kernel(nt, nd, cuts, rows1, d_proj, d_gates, w_mix, w_gates, tokens, gain, d_resid, grads,
-                d_conv, d_rate, d_onorm, d_gain2,
-                d_tokens, g_mix, g_gates, g_cols, g_small,
+                got_gate, got_up, d_conv, d_rate, d_onorm, d_gain2,
+                d_tokens, g_mix, g_gates, g_gu, g_down, g_out, g_gain1, g_gain2, g_conv, g_rate, g_onorm,
                 gm, gg, outs, ins, send, recv, small, small_in, small_send, small_recv,
-                mix_in, mix_fwd, gate_in, gate_fwd, col_in, col_fwd, dp_send, dp_recv):
+                mix_first, mix_in, mix_fwd, gate_first, gate_in, gate_fwd, col_first, col_in, col_fwd, dp_send, dp_recv):
     rows, width = tokens.shape
     share = width // nd
     bits, tbits = log2(nd), log2(nt)
     plain, swapped = orders(bits)
     greet([("tensor", nt), ("dp", nd)])
-    shares = []
-
-    def column(i, start, stop):
-        def source(b):
-            return grads.at[start:stop, pl.ds(pl.multiple_of(b * share, share), share)]
-
+
+    def sink_of(ref, *where):
         def sink(total):
-            g_cols[start:stop, :] = total
-
-        def part(ref):
-            return ref.at[:, start:stop, :]
-
-        return Share(source, sink, None, part(col_in), part(col_fwd), nd,
-                     swapped if i == 0 else plain, dp_send.at[i], dp_recv.at[i])
-
-    for i, (start, stop) in enumerate(cuts):
-        shares.append(column(i, start, stop))
-    count = len(shares)
-
-    def mix_sink(total):
-        g_mix[...] = total
-
-    def gates_sink(total):
-        g_gates[...] = total
-
-    mix_share = Share(lambda b: gm.at[b], mix_sink, None, mix_in, mix_fwd, nd, plain, dp_send.at[count], dp_recv.at[count])
-    gates_share = Share(lambda b: gg.at[b], gates_sink, None, gate_in, gate_fwd, nd, plain, dp_send.at[count + 1], dp_recv.at[count + 1])
-    for one in shares:
-        one.run(0)
+            ref[where if where else ...] = total
+
+        return sink
+
+    def column(i, sink, order, first):
+        start, stop = cuts[i]
+        got = first is not None
+        base = cuts[2][0]
+        if not got:
+            first = col_first.at[:, start - base : stop - base, :]
+        return Share(columns_of(grads, start, stop, share), sink, first, col_in.at[:, start:stop, :], col_fwd.at[:, start:stop, :],
+                     nd, order, dp_send.at[i], dp_recv.at[i], got)
+
+    gate_share = column(0, sink_of(g_gu, 0), swapped, got_gate)
+    up_share = column(1, sink_of(g_gu, 1), plain, got_up)
+    down_share = column(2, sink_of(g_down), swapped, None)
+    out_share = column(3, sink_of(g_out), plain, None)
+    mix_share = Share(lambda b: gm.at[b], sink_of(g_mix), mix_first, mix_in, mix_fwd, nd, plain, dp_send.at[4], dp_recv.at[4])
+    gates_share = Share(lambda b: gg.at[b], sink_of(g_gates), gate_first, gate_in, gate_fwd, nd, plain, dp_send.at[5], dp_recv.at[5])
+    gate_share.run(1)
+    down_share.run(0)
+    out_share.run(0)
+    up_share.run(1)
 
     def block(m):
         return pl.ds(pl.multiple_of(flip(lax.axis_index("tensor"), m) * rows, rows), rows)
@@ -750,7 +769,6 @@
         return carry
 
     lax.fori_loop(0, nd, fill, 0)
-    shares = shares[:-1] + [mix_share, shares[-1], gates_share]
     mix_share.run(0)
     gates_share.run(0)
 
@@ -791,30 +809,30 @@
     for i in range(tbits):
         small_finish(i)
         small_start(i + 1)
+    plan = [(gate_share, 2), (up_share, 2), (down_share, 1), (out_share, 1), (gate_share, 3), (up_share, 3), "small",
+            (out_share, 2), (down_share, 2), (mix_share, 1), "small", (gates_share, 1), (out_share, 3), (down_share, 3),
+            (mix_share, 2), (gates_share, 2), "small", (mix_share, 3), (gates_share, 3)]
     pending = tbits
-    for step in range(len(shares) + bits - 1):
-        for s in reversed(range(1, bits)):
-            a = step - (s - 1)
-            if 0 <= a < len(shares):
-                shares[a].run(s)
-        a = step - (bits - 1)
-        if 0 <= a < len(shares):
-            shares[a].run(bits)
-        if step >= 1 and pending < len(hops):
+    for what in plan:
+        if what == "small":
             small_finish(pending)
             pending += 1
             if pending < len(hops):
                 small_start(pending)
-    while pending < len(hops):
-        small_finish(pending)
-        pending += 1
-        if pending < len(hops):
-            small_start(pending)
-    g_small[...] = small[len(hops)]
+        else:
+            what[0].run(what[1])
+    last = small.at[len(hops)]
+    mine = pl.ds(pl.multiple_of(lax.axis_index("dp") * share, share), share)
+    g_gain1[...] = last[0:1, mine]
+    g_gain2[...] = last[1:2, mine]
+    for h in range(heads):
+        g_onorm[h : h + 1, :] = last[2:3, h * value : (h + 1) * value]
+        g_rate[h : h + 1, :] = last[3:4, h * LANES : (h + 1) * LANES]
+    g_conv[...] = last[4 : 4 + conv_rows, 0:conv_width]
     for i in range(len(hops)):
         small_copy(i).wait_send()
     norming.close()
-    for one in shares:
+    for one in (gate_share, up_share, down_share, out_share, mix_share, gates_share):
         one.close()
 
 
@@ -886,43 +904,46 @@
     mixer_args = (proj, gates_pre, aux, conv_w.reshape(4, -1), decay_rate[None, :], onorm_gain)
     mixed, states, inverses = mixer_forward(*mixer_args, dims, seqs)
     block = pltpu.VMEM((total, hidden), BF16)
-    output, d_resid2, d_gain2, d_heads, grads = call(
-        functools.partial(middle_kernel, nt),
+    share = width // nd
+    ring = share % LANES == 0 and nd == 8
+    output, d_resid2, d_gain2, d_heads, grads, *got = call(
+        functools.partial(middle_kernel, nt, nd, ring),
         [((rows, width), BF16), ((rows, width), F32), ((1, width), F32), ((total, heads * value), F32),
-         ((3 * hidden + heads * value, width), BF16)],
+         ((3 * hidden + heads * value, width), BF16)] + [((nd // 2, hidden, share), BF16)] * (2 if ring else 0),
         [pltpu.VMEM((total, width), BF16), pltpu.VMEM((total, width), BF16), pltpu.VMEM((rows, width), F32),
          pltpu.VMEM((total, hidden), F32), block, block, block,
-         pltpu.VMEM((3, nt, rows, width), BF16), pltpu.VMEM((3, nt, rows, width), BF16), dma((5, nt)), dma((5, nt))],
+         pltpu.VMEM((3, nt, rows, width), BF16), pltpu.VMEM((3, nt, rows, width), BF16), dma((5, nt)), dma((5, nt)), dma((2, nd)), dma((2, nd))],
         "middle", 1, (mixed, cots, tokens, cotangent, gain2, out2d, gu, w_down),
     )
     d_proj, d_gates, d_conv, d_rate, d_onorm = mixer_backward(*mixer_args, states, inverses, d_heads, dims, seqs)
-    share = width // nd
     exit_args = (rows1, d_proj, d_gates, mix2d, gates2d, tokens, gain1, d_resid2)
     half = pltpu.VMEM((nt, rows, width), BF16)
     ends = [0, hidden, 2 * hidden, 3 * hidden, 3 * hidden + heads * value]
-    if share % LANES == 0 and nd > 1 and nd & (nd - 1) == 0:
+    if ring:
         cuts = tuple(zip(ends[:-1], ends[1:]))
         cols = ends[-1]
         place = max(width, heads * conv)
         hops = log2(nt) + log2(nd)
         mix = heads * mix_cols
-        grad_tokens, g_mix, g_gates, g_cols, g_small = call(
+        half_nd = nd // 2
+
+        def slots(*shape):
+            return [pltpu.VMEM((n,) + shape, BF16) for n in (half_nd, half_nd - 1, half_nd - 1)]
+
+        (grad_tokens, g_mix, g_gates, g_gu, g_down, g_out, gain1_total, gain2_total, grad_conv, grad_rate, grad_onorm) = call(
             functools.partial(exit_kernel, nt, nd, cuts),
-            [((rows, width), BF16), ((share, mix), F32), ((share, LANES), F32), ((cols, share), F32), ((8, place), F32)],
+            [((rows, width), BF16), ((share, mix), F32), ((share, LANES), F32), ((2, hidden, share), F32), ((hidden, share), F32),
+             ((heads * value, share), F32), ((1, share), F32), ((1, share), F32), ((4, heads * conv), F32), ((heads, LANES), F32),
+             ((heads, value), F32)],
             [pltpu.VMEM((nd, share, mix), BF16), pltpu.VMEM((nd, share, LANES), BF16), half, half, dma((nt,)), dma((nt,)),
              pltpu.VMEM((hops + 1, 8, place), F32), pltpu.VMEM((hops, 8, place), F32), dma((hops,)), dma((hops,)),
-             pltpu.VMEM((nd - 1, share, mix), BF16), pltpu.VMEM((nd // 2 - 1, share, mix), BF16),
-             pltpu.VMEM((nd - 1, share, LANES), BF16), pltpu.VMEM((nd // 2 - 1, share, LANES), BF16),
-             pltpu.VMEM((nd - 1, cols, share), BF16), pltpu.VMEM((nd // 2 - 1, cols, share), BF16),
-             dma((len(cuts) + 2, nd)), dma((len(cuts) + 2, nd))],
-            "exit", 2, exit_args + (grads, d_conv, d_rate, d_onorm, d_gain2),
-        )
-        at = lax.axis_index("dp") * share
-        gain1_total = lax.dynamic_slice(g_small[0, :width], (at,), (share,))
-        gain2_total = lax.dynamic_slice(g_small[1, :width], (at,), (share,))
-        grad_onorm = g_small[2, : heads * value].reshape(heads, value)
-        grad_rate = g_small[3, : heads * LANES].reshape(heads, LANES)[:, 0]
-        grad_conv = g_small[4:8, : heads * conv].reshape(conv_w.shape)
+             *slots(share, mix), *slots(share, LANES),
+             pltpu.VMEM((half_nd, cols - ends[2], share), BF16), *slots(cols, share)[1:],
+             dma((6, nd)), dma((6, nd))],
+            "exit", 2, exit_args + (grads, *got, d_conv, d_rate, d_onorm, d_gain2),
+        )
+        gain1_total, gain2_total, grad_rate = gain1_total[0], gain2_total[0], grad_rate[:, 0]
+        grad_conv = grad_conv.reshape(conv_w.shape)
     else:
         grad_tokens, gain1_part, gm, gg = call(
             functools.partial(exit_plain_kernel, nt),
@@ -934,6 +955,8 @@
         g_mix = scatter(gm, scatter_dimension=0).astype(F32)
         g_gates = scatter(gg, scatter_dimension=0).astype(F32)
         g_cols = scatter(grads, scatter_dimension=1).astype(F32)
+        g_gu = g_cols[: ends[2]].reshape(2, hidden, -1)
+        g_down, g_out = g_cols[ends[2] : ends[3]], g_cols[ends[3] :]
         gain1_total, gain2_total = lax.psum(
             (scatter(gain1_part[0], scatter_dimension=0), scatter(d_gain2[0], scatter_dimension=0)), "tensor"
         )
@@ -947,10 +970,10 @@
         grad_conv,
         grad_rate,
         grad_onorm,
-        g_cols[ends[3] : ends[4]].reshape(heads, value, -1),
+        g_out.reshape(heads, value, -1),
         gain2_total,
-        jnp.transpose(g_cols[: ends[2]].reshape(2, hidden, -1), (2, 0, 1)),
-        g_cols[ends[2] : ends[3]],
+        jnp.transpose(g_gu, (2, 0, 1)),
+        g_down,
     )
 
 

time: 311 us -> 256 us (0.82)
  Pallas kernels: 285 us -> 228 us
    pallas_call x3, Pallas kernels: 233 us -> 176 us  [call(): pl.pallas_call(kernel, out_shape=[jax.ShapeDtypeStruct(s, d) for s, d in...]
    unnamed x15 -> x18, local copies, waits for them, and re-layouts: 6.79 us -> 14 us
    slice x8 -> x2, local copies, waits for them, and re-layouts: 8.65 us -> 1.56 us  [the longest x1 1.37 us: local(): grad_rate[:, 0]]
where the time goes in v2:
time: 256 us
  Pallas kernels  228 us (89%)
  local copies, waits for them, and re-layouts  24.3 us (9%)
    pallas_call x3, Pallas kernels, call(): pl.pallas_call(kernel, out_shape=[jax.ShapeDtypeStruct(s, d) for s, d in...  176 us
    pallas_call x1, Pallas kernels, mixer_backward(): pl.pallas_call(functools.partial(backward_kernel, dims), grid=(seqs, bloc...  27.1 us
    pallas_call x1, Pallas kernels, mixer_forward(): pl.pallas_call(functools.partial(forward_kernel, dims), grid=(seqs, block...  24.9 us
    unnamed x18, local copies, waits for them, and re-layouts  14 us

profile of v2, /device:TPU:0, one launch (start us, length us, event | category | flops | bytes accessed | tf_op | source)
XLA Modules:
  0.0 255.6 jit_solution(114372519115827685)
XLA Ops:
  0.6 0.7 fusion
  1.4 0.3 reduce-window.6
  1.7 0.2 slice_reduce_fusion
  1.9 0.2 reduce-window.9
  2.1 0.1 broadcast.51
  2.2 0.5 slice.43
  2.7 0.7 pad_add_fusion
  3.4 0.1 slice.39
  3.5 0.1 broadcast_in_dim.20
  3.6 0.1 broadcast_in_dim.21
  3.7 0.1 fusion.3
  3.8 0.7 reshape.216
  4.5 1.3 copy.42
  5.8 0.8 copy.39
  6.7 0.2 copy.38
  6.9 0.8 pad.16.w_gates
  7.6 4.1 %copy.41 = bf16[128,8,2,768]{3,1,2,0:T(8,128)(2,1)} copy(bf16[128,8,2,768]{3,2,1,0:T(2,128)(2,1)} %bitcast.38) | data formatting | bytes 6291456
  11.8 21.6 %entry.1 = (bf16[512,1024]{1,0:T(8,128)(2,1)}, bf16[512,1024]{1,0:T(8,128)(2,1)}, f32[512,1536]{1,0:T(8,128)}, f32[512,128]{1,0:T(8,128)}) custom-call(bf16[128,1024]{1,0:T(8,128)(2,1)} %tokens.5, bf16[128,1024]{1,0:T(8,128)(2,1)} %cot.3, f32[1,1024]{1,0:T(1,128)} %bitcast.53, bf16[1024,1536]{1,0:T(8,128)(2,1)} %bitcast.36, bf16[1024,128]{1,0:T(8,128)(2,1)} %pad.16.w_gates), custom_call_target="tpu_custom_call" | custom-call | tf_op jit(solution)/shard_map/entry/pallas_call | solution.py:867
  33.4 24.9 %mixer_forward.1 = (bf16[512,512]{1,0:T(8,128)(2,1)}, f32[8,256,256]{2,1,0:T(8,128)}, f32[8,128,64]{2,1,0:T(8,128)}) custom-call(f32[512,1536]{1,0:T(8,128)} %get-tuple-element.42.halo_ref.proj_ref, f32[512,1536]{1,0:T(8,128)} %get-tuple-element.42.halo_ref.proj_ref, f32[512,128]{1,0:T(8,128)} %get-tuple-element.43.gates_ref, f32[512,8]{1,0:T(8,128)} %bitcast.42, ...), custom_call_target="tpu_custom_call" | custom-call | flops 2048000000 | bytes 8388608 | tf_op jit(solution)/shard_map/mixer_forward/pallas_call | solution.py:378
  58.3 51.9 %middle.1 = (bf16[128,1024]{1,0:T(8,128)(2,1)}, f32[128,1024]{1,0:T(8,128)}, f32[1,1024]{1,0:T(1,128)}, f32[512,512]{1,0:T(8,128)}, bf16[2624,1024]{1,0:T(8,128)...) custom-call(bf16[512,512]{1,0:T(8,128)(2,1)} %get-tuple-element.44.mixed, ...), custom_call_target="tpu_custom_call" | custom-call | tf_op jit(solution)/shard_map/middle/pallas_call | solution.py:867
  110.2 27.1 %mixer_backward.1 = (bf16[512,1536]{1,0:T(8,128)(2,1)}, bf16[512,128]{1,0:T(8,128)(2,1)}, f32[4,1024]{1,0:T(4,128)}, f32[2,128]{1,0:T(2,128)}, f32[2,256]{1,0:T(2,128)}) custom-call(f32[512,1536]{1,0:T(8,128)} %get-tuple-element.42.halo_ref.proj_ref, f32[512,1536]{1,0:T(8,128)} %get-tuple-element.42.halo_ref.proj_ref, ...), custom_call_target="tpu_custom_call" | custom-call | flops 5120000000 | bytes 12582912 | tf_op jit(solution)/shard_map/mixer_backward/pallas_call | solution.py:405
  137.4 0.0 copy-start.2
  137.4 102.9 %exit.1 = (bf16[128,1024]{1,0:T(8,128)(2,1)}, f32[128,1536]{1,0:T(8,128)}, f32[128,128]{1,0:T(8,128)}, f32[2,704,128]{2,1,0:T(8,128)}, f32[704,128]{1,0:T(8,128)...) custom-call(bf16[512,1024]{1,0:T(8,128)(2,1)} %get-tuple-element.47., ...), custom_call_target="tpu_custom_call" | custom-call | tf_op jit(solution)/shard_map/exit/pallas_call | solution.py:867
  240.3 0.0 copy-start.3
  240.3 0.0 copy-start
  240.3 0.0 copy-start.1
  240.3 1.4 slice_reduce_fusion.1
  241.7 1.5 copy.40
  243.2 1.3 reshape.228
  244.5 2.5 reshape.226
  247.1 0.0 copy-done.2
  247.1 0.7 copy.51
  247.8 1.7 copy.52
  249.4 1.1 copy.53
  250.6 1.3 copy.54
  251.8 1.7 copy.55
  253.5 0.0 copy-done.3
  253.5 0.5 copy.56
  254.0 0.0 copy-done
  254.0 0.9 copy.57
  254.9 0.0 copy-done.1
  254.9 0.7 copy.58
  (8 shorter events, 0.1 us)
Async XLA Ops:
  137.4 109.7 %copy-start.2 = (bf16[128,1024]{1,0:T(8,128)(2,1)S(1)}, bf16[128,1024]{1,0:T(8,128)(2,1)}, u32[]{:S(2)}) copy-start(bf16[128,1024]{1,0:T(8,128)(2,1)} %get-tuple-element.99) | copy-start | bytes 786436
  240.3 13.2 %copy-start.3 = (f32[1,128]{1,0:T(1,128)S(1)}, f32[1,128]{1,0:T(1,128)}, u32[]{:S(2)}) copy-start(f32[1,128]{1,0:T(1,128)} %get-tuple-element.69) | copy-start | bytes 1540
  240.3 13.7 %copy-start = (f32[2,704,128]{2,1,0:T(8,128)S(1)}, f32[2,704,128]{2,1,0:T(8,128)}, u32[]{:S(2)}) copy-start(f32[2,704,128]{2,1,0:T(8,128)} %get-tuple-element.70) | copy-start | bytes 2162692
  240.3 14.6 %copy-start.1 = (f32[704,128]{1,0:T(8,128)S(1)}, f32[704,128]{1,0:T(8,128)}, u32[]{:S(2)}) copy-start(f32[704,128]{1,0:T(8,128)} %get-tuple-element.110) | copy-start | bytes 1081348

commit v3 on v2

--- a/solution.py
+++ b/solution.py
@@ -582,7 +582,7 @@
 
 def middle_kernel(nt, nd, ring, mixed, cots, tokens, cot, gain, w_out, w_gu, w_down,
                   out, d_resid, d_gain, d_heads, grads, *rest):
-    got = rest[:2] if ring else ()
+    got = rest[:4] if ring else ()
     rows2, drows, resid, d_act, act, d_gate, d_up, outs, ins, send, recv, dp_send, dp_recv = rest[len(got) :]
     rows = tokens.shape[0]
     hidden = w_down.shape[0]
@@ -629,7 +629,9 @@
         share = rows2.shape[1] // nd
         for i, order in enumerate(reversed(orders(log2(nd)))):
             source = columns_of(grads, i * hidden, (i + 1) * hidden, share)
-            shares.append(Share(source, None, got[i], None, None, nd, order, dp_send.at[i], dp_recv.at[i]))
+            shares.append(Share(source, None, lambda m, i=i: got[i].at[m >> 1],
+                                lambda m, i=i: got[2 + i].at[(m >> 2) * hidden : ((m >> 2) + 1) * hidden],
+                                nd, order, dp_send.at[i], dp_recv.at[i]))
             shares[i].run(0)
     d_res, d_gain[...] = rms_back(resid[...], gain[...], norming.finish())
     d_res = cot[...].astype(F32) + d_res
@@ -646,15 +648,20 @@
         d_heads[at, :] = dot(drows[at, :], w_out[...], NT)
     grads[3 * hidden :, :] = dot(mixed[...], drows[...], TN).astype(BF16)
     out[...] = (resid[...] + closing.finish()).astype(BF16)
-    for one in shares:
-        one.receive(0)
+    for i, one in enumerate(shares):
+        one.sum_second()
+        start, stop = ((3 * hidden, grads.shape[0]), (2 * hidden, 3 * hidden))[i]
+        third = Share(columns_of(grads, start, stop, share), None, None, None, nd, orders(log2(nd))[i], None, None)
+        for m in third.stage(0):
+            place = 2 * hidden + (m >> 1) * (stop - start)
+            got[2 + i][place : place + stop - start, :] = third.ref(m)[...]
     for group in (mixing, first, norming, last, closing, *shares):
         group.close()
 
 
 class Share:
-    def __init__(self, source, sink, first, into, fwd, nd, order, send, recv, got=False):
-        self.source, self.sink, self.first, self.into, self.fwd = source, sink, first, into, fwd
+    def __init__(self, source, sink, slot, fwd, nd, order, send, recv, got=0):
+        self.source, self.sink, self.slot, self.fwd = source, sink, slot, fwd
         self.order, self.send, self.recv, self.got = order, send, recv, got
         self.bits = len(order)
         self.size = nd
@@ -671,13 +678,10 @@
         names = [m for m in range(1, self.size) if low_bit(m, self.bits) == s]
         return sorted(names, key=lambda m: -int(format(m, f"0{self.bits}b")[::-1], 2))
 
-    def slot(self, m):
-        return self.first.at[m >> 1] if m & 1 else self.into.at[(m >> 1) - 1]
-
     def copy(self, m):
         s = low_bit(m, self.bits)
         return pltpu.make_async_remote_copy(
-            src_ref=self.fwd.at[(m >> 1) - 1] if s else self.ref(m), dst_ref=self.slot(m),
+            src_ref=self.fwd(m) if s else self.ref(m), dst_ref=self.slot(m),
             send_sem=self.send.at[m], recv_sem=self.recv.at[m],
             device_id={"dp": flip(self.me, 1 << self.order[s])}, device_id_type=MESH,
         )
@@ -686,7 +690,7 @@
         total = self.ref(m)[...].astype(F32)
         for j in range(low_bit(m, self.bits)):
             slot = m + (1 << j)
-            if j or not self.got:
+            if j >= self.got:
                 self.copy(slot).wait_recv()
             total = total + self.slot(slot)[...].astype(F32)
         return total
@@ -697,14 +701,18 @@
             return
         for m in self.stage(s):
             if s:
-                self.fwd[(m >> 1) - 1] = self.total(m).astype(BF16)
+                self.fwd(m)[...] = self.total(m).astype(BF16)
             copy = self.copy(m)
             copy.start()
             self.sent.append(copy)
 
-    def receive(self, s):
-        for m in self.stage(s):
-            self.copy(m).wait_recv()
+    def sum_second(self):
+        second = self.stage(1)
+        for m in self.stage(0):
+            if m - 1 not in second:
+                self.copy(m).wait_recv()
+        for m in second:
+            self.fwd(m)[...] = self.total(m).astype(BF16)
 
     def close(self):
         for copy in self.sent:
@@ -717,10 +725,10 @@
 
 
 def exit_kernel(nt, nd, cuts, rows1, d_proj, d_gates, w_mix, w_gates, tokens, gain, d_resid, grads,
-                got_gate, got_up, d_conv, d_rate, d_onorm, d_gain2,
+                got_gate, got_up, got_x, got_z, d_conv, d_rate, d_onorm, d_gain2,
                 d_tokens, g_mix, g_gates, g_gu, g_down, g_out, g_gain1, g_gain2, g_conv, g_rate, g_onorm,
                 gm, gg, outs, ins, send, recv, small, small_in, small_send, small_recv,
-                mix_first, mix_in, mix_fwd, gate_first, gate_in, gate_fwd, col_first, col_in, col_fwd, dp_send, dp_recv):
+                mix_first, mix_in, mix_fwd, gate_first, gate_in, gate_fwd, col_in, col_fwd, dp_send, dp_recv):
     rows, width = tokens.shape
     share = width // nd
     bits, tbits = log2(nd), log2(nt)
@@ -733,25 +741,50 @@
 
         return sink
 
-    def column(i, sink, order, first):
+    hidden = cuts[0][1]
+
+    def column(i, sink, order, first, second=None):
         start, stop = cuts[i]
-        got = first is not None
-        base = cuts[2][0]
-        if not got:
-            first = col_first.at[:, start - base : stop - base, :]
-        return Share(columns_of(grads, start, stop, share), sink, first, col_in.at[:, start:stop, :], col_fwd.at[:, start:stop, :],
-                     nd, order, dp_send.at[i], dp_recv.at[i], got)
-
-    gate_share = column(0, sink_of(g_gu, 0), swapped, got_gate)
-    up_share = column(1, sink_of(g_gu, 1), plain, got_up)
-    down_share = column(2, sink_of(g_down), swapped, None)
-    out_share = column(3, sink_of(g_out), plain, None)
-    mix_share = Share(lambda b: gm.at[b], sink_of(g_mix), mix_first, mix_in, mix_fwd, nd, plain, dp_send.at[4], dp_recv.at[4])
-    gates_share = Share(lambda b: gg.at[b], sink_of(g_gates), gate_first, gate_in, gate_fwd, nd, plain, dp_send.at[5], dp_recv.at[5])
-    gate_share.run(1)
-    down_share.run(0)
-    out_share.run(0)
-    up_share.run(1)
+        size = stop - start
+
+        def slot(m):
+            if m & 1:
+                return first(m >> 1, size)
+            if second is not None and m & 2:
+                return second.at[(m >> 2) * size : ((m >> 2) + 1) * size]
+            return col_in.at[(m >> 1) - 1, start:stop]
+
+        return Share(columns_of(grads, start, stop, share), sink, slot, lambda m: col_fwd.at[(m >> 1) - 1, start:stop], nd, order,
+                     dp_send.at[i], dp_recv.at[i], 1 if second is None else 2)
+
+    def after(ref):
+        return lambda k, size: ref.at[2 * hidden + k * size : 2 * hidden + (k + 1) * size]
+
+    def whole(i, source, sink, first, into, fwd, order):
+        return Share(source, sink, lambda m: first(m >> 1) if m & 1 else into((m >> 1) - 1), lambda m: fwd((m >> 1) - 1), nd, order,
+                     dp_send.at[i], dp_recv.at[i])
+
+    def mix_half(i, order):
+        width = g_mix.shape[1] // 2
+        cols = slice(i * width, (i + 1) * width)
+
+        def at(ref):
+            return lambda k: ref.at[k, :, cols]
+
+        return whole(4 + i, at(gm), sink_of(g_mix, slice(None), cols), at(mix_first), at(mix_in), at(mix_fwd), order)
+
+    gate_share = column(0, sink_of(g_gu, 0), swapped, lambda k, size: got_gate.at[k], got_x)
+    up_share = column(1, sink_of(g_gu, 1), plain, lambda k, size: got_up.at[k], got_z)
+    down_share = column(2, sink_of(g_down), swapped, after(got_z))
+    out_share = column(3, sink_of(g_out), plain, after(got_x))
+    mix0 = mix_half(0, plain)
+    mix1 = mix_half(1, swapped)
+    gates_share = whole(6, lambda b: gg.at[b], sink_of(g_gates), lambda k: gate_first.at[k], lambda k: gate_in.at[k],
+                        lambda k: gate_fwd.at[k], plain)
+    gate_share.run(2)
+    up_share.run(2)
+    down_share.run(1)
+    out_share.run(1)
 
     def block(m):
         return pl.ds(pl.multiple_of(flip(lax.axis_index("tensor"), m) * rows, rows), rows)
@@ -769,7 +802,8 @@
         return carry
 
     lax.fori_loop(0, nd, fill, 0)
-    mix_share.run(0)
+    mix0.run(0)
+    mix1.run(0)
     gates_share.run(0)
 
     d_res, gain_part = rms_back(tokens[...].astype(F32), gain[...], norming.finish())
@@ -809,9 +843,9 @@
     for i in range(tbits):
         small_finish(i)
         small_start(i + 1)
-    plan = [(gate_share, 2), (up_share, 2), (down_share, 1), (out_share, 1), (gate_share, 3), (up_share, 3), "small",
-            (out_share, 2), (down_share, 2), (mix_share, 1), "small", (gates_share, 1), (out_share, 3), (down_share, 3),
-            (mix_share, 2), (gates_share, 2), "small", (mix_share, 3), (gates_share, 3)]
+    plan = [(out_share, 2), (mix0, 1), "small", (down_share, 2), (mix1, 1), (mix0, 2), "small", (out_share, 3), (down_share, 3),
+            (gates_share, 1), (mix1, 2), (up_share, 3), (gate_share, 3), "small", (gates_share, 2), (mix0, 3), (mix1, 3),
+            (gates_share, 3)]
     pending = tbits
     for what in plan:
         if what == "small":
@@ -832,7 +866,7 @@
     for i in range(len(hops)):
         small_copy(i).wait_send()
     norming.close()
-    for one in (gate_share, up_share, down_share, out_share, mix_share, gates_share):
+    for one in (gate_share, up_share, down_share, out_share, mix0, mix1, gates_share):
         one.close()
 
 
@@ -905,16 +939,19 @@
     mixed, states, inverses = mixer_forward(*mixer_args, dims, seqs)
     block = pltpu.VMEM((total, hidden), BF16)
     share = width // nd
-    ring = share % LANES == 0 and nd == 8
+    ring = share % LANES == 0 and nd == 8 and (heads * mix_cols) % (2 * LANES) == 0
+    sends = [2 * hidden + (nd // 2) * n for n in (heads * value, hidden)]
     output, d_resid2, d_gain2, d_heads, grads, *got = call(
         functools.partial(middle_kernel, nt, nd, ring),
         [((rows, width), BF16), ((rows, width), F32), ((1, width), F32), ((total, heads * value), F32),
-         ((3 * hidden + heads * value, width), BF16)] + [((nd // 2, hidden, share), BF16)] * (2 if ring else 0),
+         ((3 * hidden + heads * value, width), BF16)] + ([((nd // 2, hidden, share), BF16)] * 2 + [((n, share), BF16) for n in sends] if ring else []),
         [pltpu.VMEM((total, width), BF16), pltpu.VMEM((total, width), BF16), pltpu.VMEM((rows, width), F32),
          pltpu.VMEM((total, hidden), F32), block, block, block,
          pltpu.VMEM((3, nt, rows, width), BF16), pltpu.VMEM((3, nt, rows, width), BF16), dma((5, nt)), dma((5, nt)), dma((2, nd)), dma((2, nd))],
         "middle", 1, (mixed, cots, tokens, cotangent, gain2, out2d, gu, w_down),
     )
+    if ring:
+        got[2:] = [lax.ppermute(x, "dp", [(i, i ^ k) for i in range(nd)]) for x, k in zip(got[2:], (1, 2))]
     d_proj, d_gates, d_conv, d_rate, d_onorm = mixer_backward(*mixer_args, states, inverses, d_heads, dims, seqs)
     exit_args = (rows1, d_proj, d_gates, mix2d, gates2d, tokens, gain1, d_resid2)
     half = pltpu.VMEM((nt, rows, width), BF16)
@@ -938,8 +975,7 @@
             [pltpu.VMEM((nd, share, mix), BF16), pltpu.VMEM((nd, share, LANES), BF16), half, half, dma((nt,)), dma((nt,)),
              pltpu.VMEM((hops + 1, 8, place), F32), pltpu.VMEM((hops, 8, place), F32), dma((hops,)), dma((hops,)),
              *slots(share, mix), *slots(share, LANES),
-             pltpu.VMEM((half_nd, cols - ends[2], share), BF16), *slots(cols, share)[1:],
-             dma((6, nd)), dma((6, nd))],
+             *slots(cols, share)[1:], dma((7, nd)), dma((7, nd))],
             "exit", 2, exit_args + (grads, *got, d_conv, d_rate, d_onorm, d_gain2),
         )
         gain1_total, gain2_total, grad_rate = gain1_total[0], gain2_total[0], grad_rate[:, 0]

time: 256 us -> 231 us (0.902)
  Pallas kernels: 228 us -> 200 us
  starting transfers between devices: 0 us -> 3.1 us
    pallas_call x3, Pallas kernels: 176 us -> 148 us  [call(): pl.pallas_call(kernel, out_shape=[jax.ShapeDtypeStruct(s, d) for s, d in...]
    ppermute x0 -> x2, starting transfers between devices: none -> 3.1 us  [local(): lax.ppermute(x, 'dp', [(i, i ^ k) for i in range(nd)])]
    unnamed x18 -> x24, local copies, waits for them, and re-layouts: 14 us -> 14.4 us
  transfers between devices with their start and end apart: 0 -> 2, of which waited for: 0 -> 0; matrix products, arithmetic and copies ran while one was open for 0% -> 0% of each run, Pallas kernels for 0% -> 12%
where the time goes in v3:
time: 231 us
  Pallas kernels  200 us (87%)
  local copies, waits for them, and re-layouts  24.7 us (11%)
  starting transfers between devices  3.1 us (1%)
    pallas_call x3, Pallas kernels, call(): pl.pallas_call(kernel, out_shape=[jax.ShapeDtypeStruct(s, d) for s, d in...  148 us
    pallas_call x1, Pallas kernels, mixer_backward(): pl.pallas_call(functools.partial(backward_kernel, dims), grid=(seqs, bloc...  27.1 us
    pallas_call x1, Pallas kernels, mixer_forward(): pl.pallas_call(functools.partial(forward_kernel, dims), grid=(seqs, block...  24.9 us
    unnamed x24, local copies, waits for them, and re-layouts  14.4 us
  transfers between devices with their start and end apart: 2, of which 0 were waited for; matrix products, arithmetic and copies ran while one was open for 0% of the time, Pallas kernels for 12%

profile of v3, /device:TPU:0, one launch (start us, length us, event | category | flops | bytes accessed | tf_op | source)
XLA Modules:
  0.0 230.8 jit_solution(467304887886127700)
XLA Ops:
  0.6 0.7 fusion
  1.4 0.3 reduce-window.6
  1.7 0.2 slice_reduce_fusion
  1.9 0.2 reduce-window.9
  2.1 0.1 broadcast.51
  2.2 0.5 slice.43
  2.7 0.1 fusion.3
  2.8 0.7 pad_add_fusion
  3.5 0.1 slice.39
  3.6 0.1 broadcast_in_dim.20
  3.7 0.1 broadcast_in_dim.21
  3.8 0.7 reshape.216
  4.5 1.3 copy.42
  5.8 0.8 copy.39
  6.7 0.2 copy.38
  6.9 4.2 %copy.41 = bf16[128,8,2,768]{3,1,2,0:T(8,128)(2,1)} copy(bf16[128,8,2,768]{3,2,1,0:T(2,128)(2,1)} %bitcast.38) | data formatting | bytes 6291456
  11.0 0.8 pad.16.w_gates
  11.8 21.6 %entry.1 = (bf16[512,1024]{1,0:T(8,128)(2,1)}, bf16[512,1024]{1,0:T(8,128)(2,1)}, f32[512,1536]{1,0:T(8,128)}, f32[512,128]{1,0:T(8,128)}) custom-call(bf16[128,1024]{1,0:T(8,128)(2,1)} %tokens.5, bf16[128,1024]{1,0:T(8,128)(2,1)} %cot.3, f32[1,1024]{1,0:T(1,128)} %bitcast.53, bf16[1024,1536]{1,0:T(8,128)(2,1)} %bitcast.36, bf16[1024,128]{1,0:T(8,128)(2,1)} %pad.16.w_gates), custom_call_target="tpu_custom_call" | custom-call | tf_op jit(solution)/shard_map/entry/pallas_call | solution.py:901
  33.3 24.9 %mixer_forward.1 = (bf16[512,512]{1,0:T(8,128)(2,1)}, f32[8,256,256]{2,1,0:T(8,128)}, f32[8,128,64]{2,1,0:T(8,128)}) custom-call(f32[512,1536]{1,0:T(8,128)} %get-tuple-element.44.halo_ref.proj_ref, f32[512,1536]{1,0:T(8,128)} %get-tuple-element.44.halo_ref.proj_ref, f32[512,128]{1,0:T(8,128)} %get-tuple-element.45.gates_ref, f32[512,8]{1,0:T(8,128)} %bitcast.42, ...), custom_call_target="tpu_custom_call" | custom-call | flops 2048000000 | bytes 8388608 | tf_op jit(solution)/shard_map/mixer_forward/pallas_call | solution.py:378
  58.3 53.1 %middle.1 = (bf16[128,1024]{1,0:T(8,128)(2,1)}, f32[128,1024]{1,0:T(8,128)}, f32[1,1024]{1,0:T(1,128)}, f32[512,512]{1,0:T(8,128)}, bf16[2624,1024]{1,0:T(8,128)...) custom-call(bf16[512,512]{1,0:T(8,128)(2,1)} %get-tuple-element.46.m, ...), custom_call_target="tpu_custom_call" | custom-call | tf_op jit(solution)/shard_map/middle/pallas_call | solution.py:901
  111.4 1.6 collective-permute-start.1
  113.0 1.5 collective-permute-start
  114.5 27.1 %mixer_backward.1 = (bf16[512,1536]{1,0:T(8,128)(2,1)}, bf16[512,128]{1,0:T(8,128)(2,1)}, f32[4,1024]{1,0:T(4,128)}, f32[2,128]{1,0:T(2,128)}, f32[2,256]{1,0:T(2,128)}) custom-call(f32[512,1536]{1,0:T(8,128)} %get-tuple-element.44.halo_ref.proj_ref, f32[512,1536]{1,0:T(8,128)} %get-tuple-element.44.halo_ref.proj_ref, ...), custom_call_target="tpu_custom_call" | custom-call | flops 5120000000 | bytes 12582912 | tf_op jit(solution)/shard_map/mixer_backward/pallas_call | solution.py:405
  141.6 0.0 collective-permute-done.got_x
  141.6 0.0 copy-start.1
  141.6 0.0 collective-permute-done.1.got_z
  141.7 0.0 copy-start
  141.7 0.9 copy-done.1
  142.6 0.4 copy-done
  143.0 0.0 copy-start.4
  143.0 73.5 %exit.1 = (bf16[128,1024]{1,0:T(8,128)(2,1)}, f32[128,1536]{1,0:T(8,128)}, f32[128,128]{1,0:T(8,128)}, f32[2,704,128]{2,1,0:T(8,128)}, f32[704,128]{1,0:T(8,128)...) custom-call(bf16[512,1024]{1,0:T(8,128)(2,1)} %get-tuple-element.49., ...), custom_call_target="tpu_custom_call" | custom-call | tf_op jit(solution)/shard_map/exit/pallas_call | solution.py:901
  216.5 0.0 copy-start.5
  216.5 0.0 copy-start.6
  216.5 0.0 copy-start.2
  216.5 0.0 copy-start.3
  216.5 1.4 slice_reduce_fusion.1
  217.9 1.5 copy.40
  219.4 1.3 reshape.228
  220.7 2.5 %reshape.226 = f32[128,2,768]{2,1,0:T(2,128)} reshape(f32[128,1536]{1,0:T(8,128)} %get-tuple-element.67) | data formatting | bytes 1572864 | tf_op jit(solution)/shard_map/reshape | solution.py:1004
  223.3 0.0 copy-done.4
  223.3 0.7 copy.51
  224.0 1.7 copy.52
  225.6 1.2 copy.53
  226.8 1.2 copy.54
  228.0 0.0 copy-done.5
  228.0 0.7 copy.55
  228.7 0.0 copy-done.6
  228.7 0.5 copy.56
  229.2 0.0 copy-done.2
  229.2 0.9 copy.57
  230.1 0.0 copy-done.3
  230.1 0.7 copy.58
  (8 shorter events, 0.1 us)
Async XLA Ops:
  111.4 30.3 %collective-permute-start.1 = (bf16[4224,128]{1,0:T(8,128)(2,1)}, bf16[4224,128]{1,0:T(8,128)(2,1)S(1)}, u32[]{:S(2)}, u32[]{:S(2)}) collective-permute-start(bf16[4224,128]{1,0:T(8,128)(2,1)} %get-tuple-element.60), channel_id=1, source_target_pairs={{0,8},{4,12},{8,0},{12,4},{16,24},{20,28},{24,16},{28,20},{1,9},{5... | collective-permute-start | bytes 3244040 | tf_op jit(solution)/shard_map/ppermute | solution.py:954
  113.0 28.6 %collective-permute-start = (bf16[3456,128]{1,0:T(8,128)(2,1)}, bf16[3456,128]{1,0:T(8,128)(2,1)S(1)}, u32[]{:S(2)}, u32[]{:S(2)}) collective-permute-start(bf16[3456,128]{1,0:T(8,128)(2,1)} %get-tuple-element.59), channel_id=1, source_target_pairs={{0,4},{4,0},{8,12},{12,8},{16,20},{20,16},{24,28},{28,24},{1,5},{5... | collective-permute-start | bytes 2654216 | tf_op jit(solution)/shard_map/ppermute | solution.py:954
  141.6 0.9 copy-start.1
  141.7 1.3 copy-start
  143.0 80.3 %copy-start.4 = (bf16[128,1024]{1,0:T(8,128)(2,1)S(1)}, bf16[128,1024]{1,0:T(8,128)(2,1)}, u32[]{:S(2)}) copy-start(bf16[128,1024]{1,0:T(8,128)(2,1)} %get-tuple-element.103) | copy-start | bytes 786436
  216.5 11.5 %copy-start.5 = (f32[512,128]{1,0:T(8,128)S(1)}, f32[512,128]{1,0:T(8,128)}, u32[]{:S(2)}) copy-start(f32[512,128]{1,0:T(8,128)} %get-tuple-element.72) | copy-start | bytes 786436
  216.5 12.2 %copy-start.6 = (f32[1,128]{1,0:T(1,128)S(1)}, f32[1,128]{1,0:T(1,128)}, u32[]{:S(2)}) copy-start(f32[1,128]{1,0:T(1,128)} %get-tuple-element.73) | copy-start | bytes 1540
  216.5 12.7 %copy-start.2 = (f32[2,704,128]{2,1,0:T(8,128)S(1)}, f32[2,704,128]{2,1,0:T(8,128)}, u32[]{:S(2)}) copy-start(f32[2,704,128]{2,1,0:T(8,128)} %get-tuple-element.74) | copy-start | bytes 2162692
  216.5 13.6 %copy-start.3 = (f32[704,128]{1,0:T(8,128)S(1)}, f32[704,128]{1,0:T(8,128)}, u32[]{:S(2)}) copy-start(f32[704,128]{1,0:T(8,128)} %get-tuple-element.114) | copy-start | bytes 1081348
